TPU v7x, 32 devices: a whole 2x2x4 slice. The times are simulated.
32 devices in a mesh: grp: 2 (over y), lon: 4 (over z), ch: 2 (over core), lat: 2 (over x).
Axes of the slice: x: 2, y: 2, z: 4, core: 2. Of those that a mesh axis runs over, the one named last changes fastest.
Arguments:
- inputs: bfloat16 [64, 512, 256], P(('grp', 'lat'), 'lon', 'ch'), parts along dimension 0, may hold values from -6 to 6
- cotangent: bfloat16 [64, 512, 256], P(('grp', 'lat'), 'lon', 'ch'), parts along dimension 0, may hold values from -6 to 6
- kernels: bfloat16 [2, 49, 256], P(None, None, 'ch'), may hold values from -0.875 to 0.875
- gains: float32 [2, 256], replicated, may hold values from 0.1 to 1.9
- w_in: bfloat16 [2, 256, 1024], P(None, None, 'ch'), may hold values from -0.375 to 0.375
- w_out: bfloat16 [2, 1024, 256], P(None, 'ch'), may hold values from -0.1875 to 0.1875
Outputs:
- grad_input: bfloat16 [64, 512, 256], P(('grp', 'lat'), 'lon', 'ch'), parts along dimension 0
- grad_w1: float32 [4, 256, 1024], P('grp', None, 'ch'), parts along dimension 0
- grad_w2: float32 [4, 1024, 256], P('grp', 'ch'), parts along dimension 0
- grad_kernel: float32 [4, 49, 256], P('grp', None, 'ch'), parts along dimension 0
There are 2 independent parts, one for each index of `grp`. A program takes and returns all parts, laid end to end along the dimension named above; an argument that names none is the same for every part. Nothing has to cross between parts.
All inputs are finite; a program needn't handle non-finite values.
Results may differ from a plain program's by a relative error of at most 0.008.
Values may be sent and summed in bfloat16 or wider, within the bound.
No kernel may reach another device: no remote copies, remote signals or barrier semaphores. Data moves between devices by JAX's collectives and lax.ppermute only.
A program may use at most 128 MiB of HBM per device.

v0:
```python
import math

import jax
import jax.numpy as jnp
from jax import lax
from jax.sharding import PartitionSpec as P

BF = jnp.bfloat16
F32 = jnp.float32


def halo_stage(block, axis, dim, periodic):
    count = lax.axis_size(axis)
    forward = [(i, i + 1) for i in range(count - 1)]
    if periodic:
        forward.append((count - 1, 0))
    backward = [(target, source) for source, target in forward]
    size = block.shape[dim]
    tail = lax.slice_in_dim(block, size - 12, None, axis=dim)
    head = lax.slice_in_dim(block, 0, 12, axis=dim)
    if count == 2 and not periodic:
        index = lax.axis_index(axis)
        got = lax.ppermute(jnp.where(index == 0, tail, head), axis, [(0, 1), (1, 0)])
        zero = jnp.zeros_like(got)
        low = jnp.where(index == 0, zero, got)
        high = jnp.where(index == 0, got, zero)
    else:
        low = lax.ppermute(tail, axis, forward)
        high = lax.ppermute(head, axis, backward)
    return jnp.concatenate([low, block, high], axis=dim)


def widen(source):
    return halo_stage(halo_stage(source, "lon", 1, True), "lat", 0, False)


def conv(widened, kernel_set, transposed):
    height = widened.shape[0] - 24
    breadth = widened.shape[1] - 24
    running = jnp.zeros((height, breadth, widened.shape[2]), F32)
    for row_tap in range(7):
        for col_tap in range(7):
            weights = kernel_set[7 * row_tap + col_tap].astype(F32)
            r, c = (6 - row_tap, 6 - col_tap) if transposed else (row_tap, col_tap)
            window = widened[4 * r : 4 * r + height, 4 * c : 4 * c + breadth]
            running = running + weights * window.astype(F32)
    return running


def tap_grads(widened, grad_conv):
    height, breadth = grad_conv.shape[:2]
    upstream = grad_conv.astype(F32)
    results = []
    for row_tap in range(7):
        for col_tap in range(7):
            window = widened[
                4 * row_tap : 4 * row_tap + height, 4 * col_tap : 4 * col_tap + breadth
            ]
            results.append(jnp.sum(window.astype(F32) * upstream, axis=(0, 1)))
    return jnp.stack(results)


def swap(x):
    return lax.ppermute(x, "ch", [(0, 1), (1, 0)])


def rows_of(x, which):
    half = x.shape[0] // 2
    return lax.dynamic_slice_in_dim(x, which * half, half, 0)


def to_cells(field):
    me = lax.axis_index("ch")
    theirs = swap(rows_of(field, 1 - me))
    mine = rows_of(field, me)
    both = jnp.concatenate([mine, theirs], axis=-1)
    return both.reshape(-1, both.shape[-1])


def to_field(cells, rows):
    me = lax.axis_index("ch")
    own = cells.shape[1] // 2
    theirs = swap(cells[:, own:])
    mine = cells[:, :own]
    pair = jnp.where(me == 0, jnp.concatenate([mine, theirs]), jnp.concatenate([theirs, mine]))
    return pair.reshape(rows, -1, own)


def normalize(convolved, gain_row):
    centre = jnp.mean(convolved, axis=-1, keepdims=True)
    centred = convolved - centre
    variance = jnp.mean(centred * centred, axis=-1, keepdims=True)
    inverse_std = lax.rsqrt(variance + 1e-06)
    normalised = centred * inverse_std
    return ((normalised * gain_row).astype(BF), normalised, inverse_std)


def norm_back(grad, normalised, inverse_std, gain_row):
    weighted = grad * gain_row
    centre_term = jnp.mean(weighted, axis=-1, keepdims=True)
    slope_term = jnp.mean(weighted * normalised, axis=-1, keepdims=True)
    return ((weighted - centre_term - normalised * slope_term) * inverse_std).astype(BF)


def dot(a, b, contract):
    return lax.dot_general(a, b, ((contract[0:1], contract[1:2]), ((), ())), preferred_element_type=F32)


def halving(axes):
    lon = lax.axis_size("lon")
    lat = lax.axis_size("lat")
    steps = []
    dist = 1
    while dist < lon:
        steps.append(("lon", dist))
        dist *= 2
    extra = []
    dist = 1
    while dist < lat:
        extra.append(("lat", dist))
        dist *= 2
    return steps[:1] + extra + steps[1:]


def grid_sum(part):
    steps = halving(None)

    def partner(x, axis, dist):
        count = lax.axis_size(axis)
        return lax.ppermute(x, axis, [(i, i ^ dist) for i in range(count)])

    for axis, dist in steps:
        bit = (lax.axis_index(axis) // dist) % 2
        half = part.shape[0] // 2
        keep = lax.dynamic_slice_in_dim(part, bit * half, half, 0)
        send = lax.dynamic_slice_in_dim(part, (1 - bit) * half, half, 0)
        part = keep + partner(send.astype(BF), axis, dist).astype(F32)
    part = part.astype(BF)
    for axis, dist in reversed(steps):
        bit = (lax.axis_index(axis) // dist) % 2
        got = partner(part, axis, dist)
        part = jnp.where(bit == 0, jnp.concatenate([part, got]), jnp.concatenate([got, part]))
    return part


def pick(me, own, other, axis):
    return jnp.where(
        me == 0, jnp.concatenate([own, other], axis), jnp.concatenate([other, own], axis)
    )


def on_device(inputs, cotangent, kernels, gains, w_in, w_out):
    rows = inputs.shape[0]
    own = inputs.shape[2]
    lat_total = rows * lax.axis_size("lat")
    lon_total = inputs.shape[1] * lax.axis_size("lon")
    scaling = 1.0 / math.sqrt(lat_total * lon_total)
    me = lax.axis_index("ch")

    def own_first(x, axis):
        half = x.shape[axis] // 2
        first = lax.dynamic_slice_in_dim(x, me * half, half, axis)
        second = lax.dynamic_slice_in_dim(x, (1 - me) * half, half, axis)
        return jnp.concatenate([first, second], axis)

    w_in_full = own_first(jnp.concatenate([w_in, swap(w_in)], axis=2), 1)
    w_out_full = own_first(jnp.concatenate([w_out, swap(w_out)], axis=1), 2)
    gains_full = own_first(gains, 1)

    widened0 = widen(inputs)
    conv0 = to_cells(conv(widened0, kernels[0], False).astype(BF))
    grad2 = to_cells(cotangent)
    y0, _, _ = normalize(conv0.astype(F32), gains_full[0])
    hid0 = jax.nn.gelu(dot(y0, w_in_full[0], (1, 0))).astype(BF)
    mix0 = dot(hid0, w_out_full[0], (1, 0)).astype(BF)
    current = (inputs.astype(F32) + to_field(mix0, rows).astype(F32)).astype(BF)
    widened1 = widen(current)
    conv1 = to_cells(conv(widened1, kernels[1], False).astype(BF))

    def back(b, conv_cells, grad):
        y, normalised, inverse_std = normalize(conv_cells.astype(F32), gains_full[b])
        pre = dot(y, w_in_full[b], (1, 0))
        hid, pullback = jax.vjp(jax.nn.gelu, pre)
        dwo = dot(hid.astype(BF), grad, (0, 0))
        dpre = pullback(dot(grad, w_out_full[b], (1, 1)))[0].astype(BF)
        dwi = dot(y, dpre, (0, 0))
        dy = dot(dpre, w_in_full[b], (1, 1))
        dconv = norm_back(dy, normalised, inverse_std, gains_full[b])
        return to_field(dconv, rows), dwi, dwo

    def weight_sums(dwi, dwo):
        half = dwi.shape[1] // 2
        got_i = swap(dwi[:, half:].astype(BF)).astype(F32)
        got_o = swap(dwo[half:].astype(BF)).astype(F32)
        wi = pick(me, dwi[:own, :half] + got_i[own:], dwi[own:, :half] + got_i[:own], 0)
        wo = pick(me, dwo[:half, :own] + got_o[:, own:], dwo[:half, own:] + got_o[:, :own], 1)
        cols = wo.shape[1]
        summed = grid_sum(jnp.concatenate([wi.reshape(-1, cols), wo])).astype(F32) * scaling
        return summed[: wi.size // cols].reshape(wi.shape), summed[wi.size // cols :]

    def tap_sum(dk):
        padded = jnp.pad(dk, ((0, 64 - dk.shape[0]), (0, 0)))
        return grid_sum(padded).astype(F32)[: dk.shape[0]] * scaling

    dconv1, dwi1, dwo1 = back(1, conv1, grad2)
    gwi1, gwo1 = weight_sums(dwi1, dwo1)
    gk1 = tap_sum(tap_grads(widened1, dconv1))
    grad1 = (cotangent.astype(F32) + conv(widen(dconv1), kernels[1], True)).astype(BF)
    dconv0, dwi0, dwo0 = back(0, conv0, to_cells(grad1))
    gwi0, gwo0 = weight_sums(dwi0, dwo0)
    gk0 = tap_sum(tap_grads(widened0, dconv0))
    grad0 = (grad1.astype(F32) + conv(widen(dconv0), kernels[0], True)).astype(BF)
    return (grad0, jnp.stack([gwi0, gwi1]), jnp.stack([gwo0, gwo1]), jnp.stack([gk0, gk1]))


def solution(mesh):
    return jax.shard_map(
        on_device,
        mesh=mesh,
        in_specs=(
            P(("grp", "lat"), "lon", "ch"),
            P(("grp", "lat"), "lon", "ch"),
            P(None, None, "ch"),
            P(),
            P(None, None, "ch"),
            P(None, "ch", None),
        ),
        out_specs=(
            P(("grp", "lat"), "lon", "ch"),
            P("grp", None, "ch"),
            P("grp", "ch", None),
            P("grp", None, "ch"),
        ),
        check_vma=False,
    )
```

profile of v0, /device:TPU:0, one launch (start us, length us, event | category | flops | bytes accessed | tf_op | source)
XLA Modules:
  0.0 270.5 jit_solution(9856027516347498127)
XLA Ops:
  1.6 5.1 %collective-permute-start.3 = (bf16[16,12,128]{2,1,0:T(8,128)(2,1)S(1)}, bf16[16,12,128]{2,1,0:T(8,128)(2,1)S(1)}, u32[]{:S(2)}, u32[]{:S(2)}) collective-permute-start(bf16[16,12,128]{2,1,0:T(8,128)(2,1)S(1)} %get-tuple-element.178), channel_id=1, source_target_pairs={{4,0},{8,4},{12,8},{0,12},{5,1},{9,5},{13,9},{1,13},{6,2},{10,6},{... | collective-permute-start | bytes 147464 | tf_op jit(solution)/shard_map/ppermute | solution.py:29
  7.3 1.3 bitcast_convert_fusion.96
  8.5 1.4 bitcast_convert_fusion.46
  10.1 1.4 bitcast_convert_fusion
  12.8 1.9 constant_dynamic-update-slice_fusion.5
  14.9 1.6 collective-permute-start.4
  17.1 1.5 bitcast_convert_fusion.1
  18.7 8.9 %collective-permute-done.4 = bf16[12,152,128]{2,1,0:T(8,128)(2,1)S(1)} collective-permute-done((bf16[12,152,128]{2,1,0:T(8,128)(2,1)S(1)}, bf16[12,152,128]{2,1,0:T(8,128)(2,1)S(1)}, u32[]{:S(2)}, u32[]{:S(2)}) %collective-permute-start.4) | collective-permute-done | bytes 466976 | tf_op jit(solution)/shard_map/ppermute | solution.py:23
  28.3 9.6 %fusion.263 = bf16[16,128,128]{2,1,0:T(8,128)(2,1)S(1)} fusion(bf16[16,128,128]{2,1,0:T(8,128)(2,1)S(1)} %copy-done.6, bf16[16,12,128]{2,1,0:T(8,128)(2,1)S(1)} %collective-permute-done.2, f32[128]{0:T(128)S(1)} %get-tuple-element.235, f32[128]{0:T(128)S(1)} %get-tuple-element.236, f32[128]{0:T(128)S(1)} %get-tuple-element.237, ...), kind=kLoop, calls=%fused_computation.509 | loop fusion | flops 40894464 | bytes 24715776 | tf_op jit(solution)/shard_map/convert_element_type | solution.py:171
  39.3 1.4 constant_dynamic-update-slice_fusion
  41.7 3.9 %multiply_convert_fusion.1 = (bf16[1024,1024]{1,0:T(8,128)(2,1)S(1)}, f32[1024,1024]{1,0:T(8,128)}) fusion(bf16[2,128,1024]{2,1,0:T(8,128)(2,1)S(1)} %get-tuple-element.147, bf16[2,128,1024]{2,1,0:T(8,128)(2,1)S(1)} %get-tuple-element.146, bf16[1024,128]{1,0:T(8,128)(2,1)S(1)} %bitcast.581, bf16[1024,128]{1,0:T(8,128)(2,1)S(1)} %bitcast.580, ...), kind=kOutput, calls=%fused_computation.119 | convolution fusion | flops 549453824 | bytes 7873536 | tf_op jit(solution)/shard_map/dot_general | solution.py:106
  45.6 1.3 copy-done.11
  49.8 3.9 %collective-permute-start.9 = (bf16[16,12,128]{2,1,0:T(8,128)(2,1)S(1)}, bf16[16,12,128]{2,1,0:T(8,128)(2,1)S(1)}, u32[]{:S(2)}, u32[]{:S(2)}) collective-permute-start(bf16[16,12,128]{2,1,0:T(8,128)(2,1)S(1)} %get-tuple-element.173), channel_id=1, source_target_pairs={{4,0},{8,4},{12,8},{0,12},{5,1},{9,5},{13,9},{1,13},{6,2},{10,6},{... | collective-permute-start | bytes 147464 | tf_op jit(solution)/shard_map/ppermute | solution.py:29
  53.7 2.7 collective-permute-done.8
  56.6 1.6 collective-permute-start.10
  60.0 9.0 %collective-permute-done.10 = bf16[12,152,128]{2,1,0:T(8,128)(2,1)S(1)} collective-permute-done((bf16[12,152,128]{2,1,0:T(8,128)(2,1)S(1)}, bf16[12,152,128]{2,1,0:T(8,128)(2,1)S(1)}, u32[]{:S(2)}, u32[]{:S(2)}) %collective-permute-start.10) | collective-permute-done | bytes 466976 | tf_op jit(solution)/shard_map/ppermute | solution.py:23
  69.9 10.4 %fusion.262 = bf16[16,128,128]{2,1,0:T(8,128)(2,1)S(1)} fusion(bf16[16,128,128]{2,1,0:T(8,128)(2,1)S(1)} %fusion.111, bf16[16,12,128]{2,1,0:T(8,128)(2,1)S(1)} %collective-permute-done.9, bf16[16,12,128]{2,1,0:T(8,128)(2,1)S(1)} %collective-permute-done.8, f32[128]{0:T(128)S(1)} %copy-done.135, f32[128]{0:T(128)S(1)} %copy-done.137, ...), kind=kLoop, calls=%fused_computation.508 | loop fusion | flops 43253760 | bytes 23192064 | tf_op jit(solution)/shard_map/convert_element_type | solution.py:178
  84.1 1.3 multiply_reduce_fusion.2
  85.4 1.7 fusion.279
  87.2 1.9 fusion.14
  89.1 3.2 %fusion.13 = bf16[1024,1024]{1,0:T(8,128)(2,1)S(1)} fusion(f32[1024,1024]{1,0:T(8,128)S(1)} %fusion.279, bf16[1024,256]{1,0:T(8,128)(2,1)S(1)} %bitcast.586, bf16[2,1024,128]{2,1,0:T(8,128)(2,1)S(1)} %copy-done.38, bf16[2,1024,128]{2,1,0:T(8,128)(2,1)S(1)} %copy-done.41), kind=kOutput, calls=%fused_computation.117 | convolution fusion | flops 558891008 | bytes 7864320 | tf_op jit(solution)/shard_map/dot_general | solution.py:106
  92.6 1.8 fusion.343
  94.4 1.8 multiply_convert_fusion.6
  97.9 4.1 %fusion.185 = (f32[128]{0:T(128)}, f32[128]{0:T(128)}, f32[128]{0:T(128)}, f32[128]{0:T(128)}, f32[128]{0:T(128)}, /*index=5*/f32[128]{0:T(128)}, f32[128]{0:T(1...) fusion(bf16[28,152,128]{2,1,0:T(8,128)(2,1)S(1)} %copy-done.1, ...), kind=kLoop, calls=%fused_computation.409 | loop fusion | flops 16774912 | bytes 10494977 | tf_op jit(solution)/shard_map/reduce_sum | solution.py:59
  102.0 14.9 %fusion.157 = (f32[128]{0:T(128)}, f32[128]{0:T(128)}, f32[128]{0:T(128)}, f32[128]{0:T(128)}, f32[128]{0:T(128)}, /*index=5*/f32[128]{0:T(128)}, f32[128]{0:T(1...) fusion(bf16[28,152,128]{2,1,0:T(8,128)(2,1)S(1)} %get-tuple-ele, ...), kind=kLoop, calls=%fused_computation.381 | loop fusion | flops 14415616 | bytes 9970688 | tf_op jit(solution)/shard_map/reduce_sum | solution.py:59
  116.9 1.3 fusion.167
  121.1 1.5 stack.425
  122.6 2.3 collective-permute-start.43
  127.8 1.2 copy.16
  129.1 1.6 collective-permute-start.44
  132.8 1.7 collective-permute-start.45
  134.5 2.0 collective-permute-start.14
  136.5 2.1 collective-permute-done.45
  138.6 3.4 %collective-permute-start.46 = (bf16[8,128]{1,0:T(8,128)(2,1)S(1)}, bf16[8,128]{1,0:T(8,128)(2,1)S(1)}, u32[]{:S(2)}, u32[]{:S(2)}) collective-permute-start(bf16[8,128]{1,0:T(8,128)(2,1)S(1)} %fusion.325), channel_id=1, source_target_pairs={{0,8},{4,12},{8,0},{12,4},{1,9},{5,13},{9,1},{13,5},{2,10},{6,14},... | collective-permute-start | bytes 6152 | tf_op jit(solution)/shard_map/ppermute | solution.py:130
  142.0 1.9 collective-permute-done.13
  144.9 1.6 collective-permute-start.15
  146.5 4.2 %collective-permute-done.32 = bf16[256,256]{0,1:T(8,128)(2,1)S(1)} collective-permute-done((bf16[256,256]{0,1:T(8,128)(2,1)S(1)}, bf16[256,256]{0,1:T(8,128)(2,1)S(1)}, u32[]{:S(2)}, u32[]{:S(2)}) %collective-permute-start.32) | collective-permute-done | bytes 131104 | tf_op jit(solution)/shard_map/ppermute | solution.py:130
  151.5 4.8 %collective-permute-done.33 = bf16[128,256]{0,1:T(8,128)(2,1)S(1)} collective-permute-done((bf16[128,256]{0,1:T(8,128)(2,1)S(1)}, bf16[128,256]{0,1:T(8,128)(2,1)S(1)}, u32[]{:S(2)}, u32[]{:S(2)}) %collective-permute-start.33) | collective-permute-done | bytes 65568 | tf_op jit(solution)/shard_map/ppermute | solution.py:130
  156.4 2.1 collective-permute-done.15
  159.9 10.1 %add_convert_fusion.1 = bf16[16,128,128]{2,1,0:T(8,128)(2,1)S(1)} fusion(bf16[16,128,128]{2,1,0:T(8,128)(2,1)S(1)} %copy-done.21, bf16[16,128,128]{2,1,0:T(8,128)(2,1)S(1)} %bitcast.574, bf16[16,12,128]{2,1,0:T(8,128)(2,1)S(1)} %collective-permute-done.13, bf16[16,12,128]{2,1,0:T(8,128)(2,1)S(1)} %collective-permute-done.14, ...), kind=kLoop, calls=%fused_computation.501 | loop fusion | flops 43778048 | bytes 23716352 | tf_op jit(solution)/shard_map/convert_element_type | solution.py:208
  170.9 3.6 %collective-permute-done.48 = bf16[32,128]{1,0:T(8,128)(2,1)S(1)} collective-permute-done((bf16[32,128]{1,0:T(8,128)(2,1)S(1)}, bf16[32,128]{1,0:T(8,128)(2,1)S(1)}, u32[]{:S(2)}, u32[]{:S(2)}) %collective-permute-start.48) | collective-permute-done | bytes 8224 | tf_op jit(solution)/shard_map/ppermute | solution.py:130
  174.6 1.6 collective-permute-done.35
  177.5 2.5 fusion.352
  180.6 3.2 %fusion.6 = bf16[1024,1024]{1,0:T(8,128)(2,1)S(1)} fusion(f32[1024,1024]{1,0:T(8,128)S(1)} %copy-done.255, bf16[1024,256]{1,0:T(8,128)(2,1)S(1)} %bitcast.583, bf16[2,1024,128]{2,1,0:T(8,128)(2,1)S(1)} %copy-done.42, bf16[2,1024,128]{2,1,0:T(8,128)(2,1)S(1)} %copy-done.39), kind=kOutput, calls=%fused_computation.110 | convolution fusion | flops 558891008 | bytes 7864320 | tf_op jit(solution)/shard_map/dot_general | solution.py:106
  184.7 1.6 fusion.342
  191.2 1.2 copy.17
  193.4 5.0 %fusion.259 = (f32[128]{0:T(128)S(1)}, f32[128]{0:T(128)S(1)}, f32[128]{0:T(128)S(1)}, f32[128]{0:T(128)S(1)}, f32[128]{0:T(128)S(1)}, /*index=5*/f32[128]{0:T(1...) fusion(bf16[28,152,128]{2,1,0:T(8,128)(2,1)S(1)} %get-tuple-ele, ...), kind=kLoop, calls=%fused_computation.483 | loop fusion | flops 16774912 | bytes 10494977 | tf_op jit(solution)/shard_map/reduce_sum | solution.py:59
  198.4 2.8 %fusion.231 = (f32[128]{0:T(128)S(1)}, f32[128]{0:T(128)S(1)}, f32[128]{0:T(128)S(1)}, f32[128]{0:T(128)S(1)}, f32[128]{0:T(128)S(1)}, /*index=5*/f32[128]{0:T(1...) fusion(bf16[28,152,128]{2,1,0:T(8,128)(2,1)S(1)} %get-tuple-ele, ...), kind=kLoop, calls=%fused_computation.455 | loop fusion | flops 14415616 | bytes 9970688 | tf_op jit(solution)/shard_map/reduce_sum | solution.py:59
  201.3 2.3 fusion.241
  203.9 2.0 collective-permute-start.37
  209.8 3.0 %collective-permute-done.38 = bf16[16,128]{1,0:T(8,128)(2,1)S(1)} collective-permute-done((bf16[16,128]{1,0:T(8,128)(2,1)S(1)}, bf16[16,128]{1,0:T(8,128)(2,1)S(1)}, u32[]{:S(2)}, u32[]{:S(2)}) %collective-permute-start.38) | collective-permute-done | bytes 4128 | tf_op jit(solution)/shard_map/ppermute | solution.py:130
  213.7 3.6 %collective-permute-done.39 = bf16[8,128]{1,0:T(8,128)(2,1)S(1)} collective-permute-done((bf16[8,128]{1,0:T(8,128)(2,1)S(1)}, bf16[8,128]{1,0:T(8,128)(2,1)S(1)}, u32[]{:S(2)}, u32[]{:S(2)}) %collective-permute-start.39) | collective-permute-done | bytes 2080 | tf_op jit(solution)/shard_map/ppermute | solution.py:130
  218.5 3.4 %collective-permute-done.40 = bf16[8,128]{1,0:T(8,128)(2,1)S(1)} collective-permute-done((bf16[8,128]{1,0:T(8,128)(2,1)S(1)}, bf16[8,128]{1,0:T(8,128)(2,1)S(1)}, u32[]{:S(2)}, u32[]{:S(2)}) %collective-permute-start.40) | collective-permute-done | bytes 2080 | tf_op jit(solution)/shard_map/ppermute | solution.py:130
  223.0 2.5 collective-permute-done.41
  225.9 1.9 collective-permute-start.19
  228.0 1.7 collective-permute-done.42
  230.4 3.5 %collective-permute-done.18 = bf16[16,12,128]{2,1,0:T(8,128)(2,1)S(1)} collective-permute-done((bf16[16,12,128]{2,1,0:T(8,128)(2,1)S(1)}, bf16[16,12,128]{2,1,0:T(8,128)(2,1)S(1)}, u32[]{:S(2)}, u32[]{:S(2)}) %collective-permute-start.18) | collective-permute-done | bytes 49184 | tf_op jit(solution)/shard_map/ppermute | solution.py:28
  234.9 1.6 collective-permute-start.20
  236.4 2.9 %collective-permute-done.24 = bf16[256,256]{0,1:T(8,128)(2,1)S(1)} collective-permute-done((bf16[256,256]{0,1:T(8,128)(2,1)S(1)}, bf16[256,256]{0,1:T(8,128)(2,1)S(1)}, u32[]{:S(2)}, u32[]{:S(2)}) %collective-permute-start.24) | collective-permute-done | bytes 131104 | tf_op jit(solution)/shard_map/ppermute | solution.py:130
  240.1 4.5 %collective-permute-done.25 = bf16[128,256]{0,1:T(8,128)(2,1)S(1)} collective-permute-done((bf16[128,256]{0,1:T(8,128)(2,1)S(1)}, bf16[128,256]{0,1:T(8,128)(2,1)S(1)}, u32[]{:S(2)}, u32[]{:S(2)}) %collective-permute-start.25) | collective-permute-done | bytes 65568 | tf_op jit(solution)/shard_map/ppermute | solution.py:130
  244.8 5.2 %collective-permute-done.26 = bf16[128,256]{0,1:T(8,128)(2,1)S(1)} collective-permute-done((bf16[128,256]{0,1:T(8,128)(2,1)S(1)}, bf16[128,256]{0,1:T(8,128)(2,1)S(1)}, u32[]{:S(2)}, u32[]{:S(2)}) %collective-permute-start.26) | collective-permute-done | bytes 65568 | tf_op jit(solution)/shard_map/ppermute | solution.py:130
  251.2 4.3 %collective-permute-done.27 = bf16[256,256]{0,1:T(8,128)(2,1)S(1)} collective-permute-done((bf16[256,256]{0,1:T(8,128)(2,1)S(1)}, bf16[256,256]{0,1:T(8,128)(2,1)S(1)}, u32[]{:S(2)}, u32[]{:S(2)}) %collective-permute-start.27) | collective-permute-done | bytes 131104 | tf_op jit(solution)/shard_map/ppermute | solution.py:130
  256.1 10.4 %add_convert_fusion = bf16[16,128,128]{2,1,0:T(8,128)(2,1)} fusion(bf16[16,128,128]{2,1,0:T(8,128)(2,1)S(1)} %add_convert_fusion.1, bf16[16,128,128]{2,1,0:T(8,128)(2,1)S(1)} %bitcast.578, bf16[16,12,128]{2,1,0:T(8,128)(2,1)S(1)} %collective-permute-done.18, bf16[16,12,128]{2,1,0:T(8,128)(2,1)S(1)} %collective-permute-done.19, ...), kind=kLoop, calls=%fused_computation.498 | loop fusion | flops 43778048 | bytes 23716352 | tf_op jit(solution)/shard_map/convert_element_type | solution.py:212
  267.6 1.3 copy.18
  (697 shorter events, 50.4 us)
Async XLA Ops:
  1.6 13.0 %collective-permute-start.3 = (bf16[16,12,128]{2,1,0:T(8,128)(2,1)S(1)}, bf16[16,12,128]{2,1,0:T(8,128)(2,1)S(1)}, u32[]{:S(2)}, u32[]{:S(2)}) collective-permute-start(bf16[16,12,128]{2,1,0:T(8,128)(2,1)S(1)} %get-tuple-element.178), channel_id=1, source_target_pairs={{4,0},{8,4},{12,8},{0,12},{5,1},{9,5},{13,9},{1,13},{6,2},{10,6},{... | collective-permute-start | bytes 147464 | tf_op jit(solution)/shard_map/ppermute | solution.py:29
  6.7 7.9 %collective-permute-start.2 = (bf16[16,12,128]{2,1,0:T(8,128)(2,1)S(1)}, bf16[16,12,128]{2,1,0:T(8,128)(2,1)S(1)}, u32[]{:S(2)}, u32[]{:S(2)}) collective-permute-start(bf16[16,12,128]{2,1,0:T(8,128)(2,1)S(1)} %get-tuple-element.179), channel_id=1, source_target_pairs={{0,4},{4,8},{8,12},{12,0},{1,5},{5,9},{9,13},{13,1},{2,6},{6,10},{... | collective-permute-start | bytes 147464 | tf_op jit(solution)/shard_map/ppermute | solution.py:28
  6.7 31.3 %collective-permute-start.6 = (bf16[2,256,512]{2,1,0:T(8,128)(2,1)}, bf16[2,256,512]{2,1,0:T(8,128)(2,1)}, u32[]{:S(2)}, u32[]{:S(2)}) collective-permute-start(bf16[2,256,512]{2,1,0:T(8,128)(2,1)} %param.10), channel_id=1, source_target_pairs={{0,2},{2,0},{1,3},{3,1},{4,6},{6,4},{5,7},{7,5},{8,10},{10,8},{9,1... | collective-permute-start | bytes 1572872 | tf_op jit(solution)/shard_map/ppermute | solution.py:64
  6.8 32.6 %collective-permute-start.1 = (bf16[2,512,256]{2,1,0:T(8,128)(2,1)}, bf16[2,512,256]{2,1,0:T(8,128)(2,1)}, u32[]{:S(2)}, u32[]{:S(2)}) collective-permute-start(bf16[2,512,256]{2,1,0:T(8,128)(2,1)} %param.11), channel_id=1, source_target_pairs={{0,2},{2,0},{1,3},{3,1},{4,6},{6,4},{5,7},{7,5},{8,10},{10,8},{9,1... | collective-permute-start | bytes 1572872 | tf_op jit(solution)/shard_map/ppermute | solution.py:64
  10.0 17.9 %copy-start.48 = (f32[128]{0:T(128)}, f32[128]{0:T(128)S(1)}, u32[]{:S(2)}) copy-start(f32[128]{0:T(128)S(1)} %get-tuple-element.235) | copy-start | bytes 1540
  10.0 17.9 %copy-start.50 = (f32[128]{0:T(128)}, f32[128]{0:T(128)S(1)}, u32[]{:S(2)}) copy-start(f32[128]{0:T(128)S(1)} %get-tuple-element.236) | copy-start | bytes 1540
  10.0 17.9 %copy-start.52 = (f32[128]{0:T(128)}, f32[128]{0:T(128)S(1)}, u32[]{:S(2)}) copy-start(f32[128]{0:T(128)S(1)} %get-tuple-element.237) | copy-start | bytes 1540
  10.0 17.9 %copy-start.54 = (f32[128]{0:T(128)}, f32[128]{0:T(128)S(1)}, u32[]{:S(2)}) copy-start(f32[128]{0:T(128)S(1)} %get-tuple-element.238) | copy-start | bytes 1540
  10.0 17.9 %copy-start.56 = (f32[128]{0:T(128)}, f32[128]{0:T(128)S(1)}, u32[]{:S(2)}) copy-start(f32[128]{0:T(128)S(1)} %get-tuple-element.239) | copy-start | bytes 1540
  10.0 17.9 %copy-start.58 = (f32[128]{0:T(128)}, f32[128]{0:T(128)S(1)}, u32[]{:S(2)}) copy-start(f32[128]{0:T(128)S(1)} %get-tuple-element.240) | copy-start | bytes 1540
  10.0 17.9 %copy-start.60 = (f32[128]{0:T(128)}, f32[128]{0:T(128)S(1)}, u32[]{:S(2)}) copy-start(f32[128]{0:T(128)S(1)} %get-tuple-element.241) | copy-start | bytes 1540
  10.0 17.9 %copy-start.62 = (f32[128]{0:T(128)}, f32[128]{0:T(128)S(1)}, u32[]{:S(2)}) copy-start(f32[128]{0:T(128)S(1)} %get-tuple-element.242) | copy-start | bytes 1540
  10.0 17.9 %copy-start.64 = (f32[128]{0:T(128)}, f32[128]{0:T(128)S(1)}, u32[]{:S(2)}) copy-start(f32[128]{0:T(128)S(1)} %get-tuple-element.243) | copy-start | bytes 1540
  10.1 17.9 %copy-start.66 = (f32[128]{0:T(128)}, f32[128]{0:T(128)S(1)}, u32[]{:S(2)}) copy-start(f32[128]{0:T(128)S(1)} %get-tuple-element.244) | copy-start | bytes 1540
  11.5 16.6 %copy-start.72 = (f32[128]{0:T(128)}, f32[128]{0:T(128)S(1)}, u32[]{:S(2)}) copy-start(f32[128]{0:T(128)S(1)} %get-tuple-element.267) | copy-start | bytes 1540
  11.5 16.6 %copy-start.74 = (f32[128]{0:T(128)}, f32[128]{0:T(128)S(1)}, u32[]{:S(2)}) copy-start(f32[128]{0:T(128)S(1)} %get-tuple-element.268) | copy-start | bytes 1540
  11.5 16.6 %copy-start.76 = (f32[128]{0:T(128)}, f32[128]{0:T(128)S(1)}, u32[]{:S(2)}) copy-start(f32[128]{0:T(128)S(1)} %get-tuple-element.269) | copy-start | bytes 1540
  14.9 12.7 %collective-permute-start.4 = (bf16[12,152,128]{2,1,0:T(8,128)(2,1)S(1)}, bf16[12,152,128]{2,1,0:T(8,128)(2,1)S(1)}, u32[]{:S(2)}, u32[]{:S(2)}) collective-permute-start(bf16[12,152,128]{2,1,0:T(8,128)(2,1)S(1)} %slice_select_fusion.3), channel_id=1, source_target_pairs={{0,1},{1,0},{2,3},{3,2},{4,5},{5,4},{6,7},{7,6},{8,9},{9,8},{10,11... | collective-permute-start | bytes 1400840 | tf_op jit(solution)/shard_map/ppermute | solution.py:23
  38.0 3.0 %collective-permute-start.5 = (bf16[8,128,128]{2,1,0:T(8,128)(2,1)S(1)}, bf16[8,128,128]{2,1,0:T(8,128)(2,1)S(1)}, u32[]{:S(2)}, u32[]{:S(2)}) collective-permute-start(bf16[8,128,128]{2,1,0:T(8,128)(2,1)S(1)} %get-tuple-element.177), channel_id=1, source_target_pairs={{0,2},{2,0},{1,3},{3,1},{4,6},{6,4},{5,7},{7,5},{8,10},{10,8},{9,1... | collective-permute-start | bytes 786440 | tf_op jit(solution)/shard_map/ppermute | solution.py:64
  47.7 1.7 collective-permute-start.7
  49.7 19.7 %copy-start.8 = (bf16[16,128,128]{2,1,0:T(8,128)(2,1)}, bf16[16,128,128]{2,1,0:T(8,128)(2,1)S(1)}, u32[]{:S(2)}) copy-start(bf16[16,128,128]{2,1,0:T(8,128)(2,1)S(1)} %fusion.111) | copy-start | bytes 1572868
  49.8 6.6 %collective-permute-start.8 = (bf16[16,12,128]{2,1,0:T(8,128)(2,1)S(1)}, bf16[16,12,128]{2,1,0:T(8,128)(2,1)S(1)}, u32[]{:S(2)}, u32[]{:S(2)}) collective-permute-start(bf16[16,12,128]{2,1,0:T(8,128)(2,1)S(1)} %get-tuple-element.172), channel_id=1, source_target_pairs={{0,4},{4,8},{8,12},{12,0},{1,5},{5,9},{9,13},{13,1},{2,6},{6,10},{... | collective-permute-start | bytes 147464 | tf_op jit(solution)/shard_map/ppermute | solution.py:28
  49.8 6.5 %collective-permute-start.9 = (bf16[16,12,128]{2,1,0:T(8,128)(2,1)S(1)}, bf16[16,12,128]{2,1,0:T(8,128)(2,1)S(1)}, u32[]{:S(2)}, u32[]{:S(2)}) collective-permute-start(bf16[16,12,128]{2,1,0:T(8,128)(2,1)S(1)} %get-tuple-element.173), channel_id=1, source_target_pairs={{4,0},{8,4},{12,8},{0,12},{5,1},{9,5},{13,9},{1,13},{6,2},{10,6},{... | collective-permute-start | bytes 147464 | tf_op jit(solution)/shard_map/ppermute | solution.py:29
  56.6 12.4 %collective-permute-start.10 = (bf16[12,152,128]{2,1,0:T(8,128)(2,1)S(1)}, bf16[12,152,128]{2,1,0:T(8,128)(2,1)S(1)}, u32[]{:S(2)}, u32[]{:S(2)}) collective-permute-start(bf16[12,152,128]{2,1,0:T(8,128)(2,1)S(1)} %slice_select_fusion.2), channel_id=1, source_target_pairs={{0,1},{1,0},{2,3},{3,2},{4,5},{5,4},{6,7},{7,6},{8,9},{9,8},{10,11... | collective-permute-start | bytes 1400840 | tf_op jit(solution)/shard_map/ppermute | solution.py:23
  59.0 22.0 %collective-permute-start = (bf16[8,128,128]{2,1,0:T(8,128)(2,1)}, bf16[8,128,128]{2,1,0:T(8,128)(2,1)}, u32[]{:S(2)}, u32[]{:S(2)}) collective-permute-start(bf16[8,128,128]{2,1,0:T(8,128)(2,1)} %get-tuple-element.169), channel_id=1, source_target_pairs={{0,2},{2,0},{1,3},{3,1},{4,6},{6,4},{5,7},{7,5},{8,10},{10,8},{9,1... | collective-permute-start | bytes 786440 | tf_op jit(solution)/shard_map/ppermute | solution.py:64
  81.0 1.9 collective-permute-start.11
  92.3 25.9 %collective-permute-start.30 = (bf16[512,256]{0,1:T(8,128)(2,1)S(1)}, bf16[512,256]{0,1:T(8,128)(2,1)S(1)}, u32[]{:S(2)}, u32[]{:S(2)}) collective-permute-start(bf16[512,256]{0,1:T(8,128)(2,1)S(1)} %slice.2794), channel_id=1, source_target_pairs={{0,2},{2,0},{1,3},{3,1},{4,6},{6,4},{5,7},{7,5},{8,10},{10,8},{9,1... | collective-permute-start | bytes 786440 | tf_op jit(solution)/shard_map/ppermute | solution.py:64
  96.3 1.6 collective-permute-start.12
  97.5 21.3 %collective-permute-start.29 = (bf16[256,512]{1,0:T(8,128)(2,1)S(1)}, bf16[256,512]{1,0:T(8,128)(2,1)S(1)}, u32[]{:S(2)}, u32[]{:S(2)}) collective-permute-start(bf16[256,512]{1,0:T(8,128)(2,1)S(1)} %slice.2795), channel_id=1, source_target_pairs={{0,2},{2,0},{1,3},{3,1},{4,6},{6,4},{5,7},{7,5},{8,10},{10,8},{9,1... | collective-permute-start | bytes 786440 | tf_op jit(solution)/shard_map/ppermute | solution.py:64
  102.0 17.6 %copy-start.2 = (bf16[2048,128]{1,0:T(8,128)(2,1)}, bf16[2048,128]{1,0:T(8,128)(2,1)S(1)}, u32[]{:S(2)}) copy-start(bf16[2048,128]{1,0:T(8,128)(2,1)S(1)} %get-tuple-element.131) | copy-start | bytes 1572868
  122.6 6.4 %collective-permute-start.43 = (bf16[32,128]{1,0:T(8,128)(2,1)S(1)}, bf16[32,128]{1,0:T(8,128)(2,1)S(1)}, u32[]{:S(2)}, u32[]{:S(2)}) collective-permute-start(bf16[32,128]{1,0:T(8,128)(2,1)S(1)} %fusion.314), channel_id=1, source_target_pairs={{0,4},{4,0},{8,12},{12,8},{1,5},{5,1},{9,13},{13,9},{2,6},{6,2},{1... | collective-permute-start | bytes 24584 | tf_op jit(solution)/shard_map/ppermute | solution.py:130
  129.1 3.7 %collective-permute-start.44 = (bf16[16,128]{1,0:T(8,128)(2,1)S(1)}, bf16[16,128]{1,0:T(8,128)(2,1)S(1)}, u32[]{:S(2)}, u32[]{:S(2)}) collective-permute-start(bf16[16,128]{1,0:T(8,128)(2,1)S(1)} %fusion.320), channel_id=1, source_target_pairs={{0,1},{1,0},{2,3},{3,2},{4,5},{5,4},{6,7},{7,6},{8,9},{9,8},{10,11... | collective-permute-start | bytes 12296 | tf_op jit(solution)/shard_map/ppermute | solution.py:130
  131.8 12.3 %collective-permute-start.31 = (bf16[512,256]{0,1:T(8,128)(2,1)S(1)}, bf16[512,256]{0,1:T(8,128)(2,1)S(1)}, u32[]{:S(2)}, u32[]{:S(2)}) collective-permute-start(bf16[512,256]{0,1:T(8,128)(2,1)S(1)} %fusion.286), channel_id=1, source_target_pairs={{0,4},{4,0},{8,12},{12,8},{1,5},{5,1},{9,13},{13,9},{2,6},{6,2},{1... | collective-permute-start | bytes 786440 | tf_op jit(solution)/shard_map/ppermute | solution.py:130
  132.8 5.9 %collective-permute-start.45 = (bf16[8,128]{1,0:T(8,128)(2,1)S(1)}, bf16[8,128]{1,0:T(8,128)(2,1)S(1)}, u32[]{:S(2)}, u32[]{:S(2)}) collective-permute-start(bf16[8,128]{1,0:T(8,128)(2,1)S(1)} %fusion.326), channel_id=1, source_target_pairs={{0,8},{4,12},{8,0},{12,4},{1,9},{5,13},{9,1},{13,5},{2,10},{6,14},... | collective-permute-start | bytes 6152 | tf_op jit(solution)/shard_map/ppermute | solution.py:130
  134.5 7.6 %collective-permute-start.14 = (bf16[16,12,128]{2,1,0:T(8,128)(2,1)S(1)}, bf16[16,12,128]{2,1,0:T(8,128)(2,1)S(1)}, u32[]{:S(2)}, u32[]{:S(2)}) collective-permute-start(bf16[16,12,128]{2,1,0:T(8,128)(2,1)S(1)} %get-tuple-element.164), channel_id=1, source_target_pairs={{4,0},{8,4},{12,8},{0,12},{5,1},{9,5},{13,9},{1,13},{6,2},{10,6},{... | collective-permute-start | bytes 147464 | tf_op jit(solution)/shard_map/ppermute | solution.py:29
  136.4 7.5 %collective-permute-start.13 = (bf16[16,12,128]{2,1,0:T(8,128)(2,1)S(1)}, bf16[16,12,128]{2,1,0:T(8,128)(2,1)S(1)}, u32[]{:S(2)}, u32[]{:S(2)}) collective-permute-start(bf16[16,12,128]{2,1,0:T(8,128)(2,1)S(1)} %get-tuple-element.165), channel_id=1, source_target_pairs={{0,4},{4,8},{8,12},{12,0},{1,5},{5,9},{9,13},{13,1},{2,6},{6,10},{... | collective-permute-start | bytes 147464 | tf_op jit(solution)/shard_map/ppermute | solution.py:28
  138.6 12.2 %collective-permute-start.46 = (bf16[8,128]{1,0:T(8,128)(2,1)S(1)}, bf16[8,128]{1,0:T(8,128)(2,1)S(1)}, u32[]{:S(2)}, u32[]{:S(2)}) collective-permute-start(bf16[8,128]{1,0:T(8,128)(2,1)S(1)} %fusion.325), channel_id=1, source_target_pairs={{0,8},{4,12},{8,0},{12,4},{1,9},{5,13},{9,1},{13,5},{2,10},{6,14},... | collective-permute-start | bytes 6152 | tf_op jit(solution)/shard_map/ppermute | solution.py:130
  144.3 6.4 %collective-permute-start.32 = (bf16[256,256]{0,1:T(8,128)(2,1)S(1)}, bf16[256,256]{0,1:T(8,128)(2,1)S(1)}, u32[]{:S(2)}, u32[]{:S(2)}) collective-permute-start(bf16[256,256]{0,1:T(8,128)(2,1)S(1)} %dynamic-slice_convert_fusion), channel_id=1, source_target_pairs={{0,1},{1,0},{2,3},{3,2},{4,5},{5,4},{6,7},{7,6},{8,9},{9,8},{10,11... | collective-permute-start | bytes 393224 | tf_op jit(solution)/shard_map/ppermute | solution.py:130
  144.9 13.5 %collective-permute-start.15 = (bf16[12,152,128]{2,1,0:T(8,128)(2,1)S(1)}, bf16[12,152,128]{2,1,0:T(8,128)(2,1)S(1)}, u32[]{:S(2)}, u32[]{:S(2)}) collective-permute-start(bf16[12,152,128]{2,1,0:T(8,128)(2,1)S(1)} %slice_select_fusion.1), channel_id=1, source_target_pairs={{0,1},{1,0},{2,3},{3,2},{4,5},{5,4},{6,7},{7,6},{8,9},{9,8},{10,11... | collective-permute-start | bytes 1400840 | tf_op jit(solution)/shard_map/ppermute | solution.py:23
  150.8 5.4 %collective-permute-start.33 = (bf16[128,256]{0,1:T(8,128)(2,1)S(1)}, bf16[128,256]{0,1:T(8,128)(2,1)S(1)}, u32[]{:S(2)}, u32[]{:S(2)}) collective-permute-start(bf16[128,256]{0,1:T(8,128)(2,1)S(1)} %dynamic-slice_convert_fusion.2), channel_id=1, source_target_pairs={{0,8},{4,12},{8,0},{12,4},{1,9},{5,13},{9,1},{13,5},{2,10},{6,14},... | collective-permute-start | bytes 196616 | tf_op jit(solution)/shard_map/ppermute | solution.py:130
  150.9 19.9 %collective-permute-start.47 = (bf16[16,128]{1,0:T(8,128)(2,1)S(1)}, bf16[16,128]{1,0:T(8,128)(2,1)S(1)}, u32[]{:S(2)}, u32[]{:S(2)}) collective-permute-start(bf16[16,128]{1,0:T(8,128)(2,1)S(1)} %maximum_select_fusion.16), channel_id=1, source_target_pairs={{0,1},{1,0},{2,3},{3,2},{4,5},{5,4},{6,7},{7,6},{8,9},{9,8},{10,11... | collective-permute-start | bytes 12296 | tf_op jit(solution)/shard_map/ppermute | solution.py:130
  156.3 13.9 %collective-permute-start.34 = (bf16[128,256]{0,1:T(8,128)(2,1)S(1)}, bf16[128,256]{0,1:T(8,128)(2,1)S(1)}, u32[]{:S(2)}, u32[]{:S(2)}) collective-permute-start(bf16[128,256]{0,1:T(8,128)(2,1)S(1)} %add_convert_fusion.2), channel_id=1, source_target_pairs={{0,8},{4,12},{8,0},{12,4},{1,9},{5,13},{9,1},{13,5},{2,10},{6,14},... | collective-permute-start | bytes 196616 | tf_op jit(solution)/shard_map/ppermute | solution.py:130
  170.1 6.3 %collective-permute-start.16 = (bf16[8,128,128]{2,1,0:T(8,128)(2,1)S(1)}, bf16[8,128,128]{2,1,0:T(8,128)(2,1)}, u32[]{:S(2)}, u32[]{:S(2)}) collective-permute-start(bf16[8,128,128]{2,1,0:T(8,128)(2,1)S(1)} %get-tuple-element.163), channel_id=1, source_target_pairs={{0,2},{2,0},{1,3},{3,1},{4,6},{6,4},{5,7},{7,5},{8,10},{10,8},{9,1... | collective-permute-start | bytes 786440 | tf_op jit(solution)/shard_map/ppermute | solution.py:64
  170.2 6.0 %collective-permute-start.35 = (bf16[256,256]{0,1:T(8,128)(2,1)S(1)}, bf16[256,256]{0,1:T(8,128)(2,1)S(1)}, u32[]{:S(2)}, u32[]{:S(2)}) collective-permute-start(bf16[256,256]{0,1:T(8,128)(2,1)S(1)} %maximum_select_fusion.12), channel_id=1, source_target_pairs={{0,1},{1,0},{2,3},{3,2},{4,5},{5,4},{6,7},{7,6},{8,9},{9,8},{10,11... | collective-permute-start | bytes 393224 | tf_op jit(solution)/shard_map/ppermute | solution.py:130
  170.8 3.7 %collective-permute-start.48 = (bf16[32,128]{1,0:T(8,128)(2,1)S(1)}, bf16[32,128]{1,0:T(8,128)(2,1)S(1)}, u32[]{:S(2)}, u32[]{:S(2)}) collective-permute-start(bf16[32,128]{1,0:T(8,128)(2,1)S(1)} %maximum_select_fusion.14), channel_id=1, source_target_pairs={{0,4},{4,0},{8,12},{12,8},{1,5},{5,1},{9,13},{13,9},{2,6},{6,2},{1... | collective-permute-start | bytes 24584 | tf_op jit(solution)/shard_map/ppermute | solution.py:130
  176.3 13.7 %collective-permute-start.36 = (bf16[512,256]{0,1:T(8,128)(2,1)S(1)}, bf16[512,256]{0,1:T(8,128)(2,1)S(1)}, u32[]{:S(2)}, u32[]{:S(2)}) collective-permute-start(bf16[512,256]{0,1:T(8,128)(2,1)S(1)} %maximum_select_fusion.10), channel_id=1, source_target_pairs={{0,4},{4,0},{8,12},{12,8},{1,5},{5,1},{9,13},{13,9},{2,6},{6,2},{1... | collective-permute-start | bytes 786440 | tf_op jit(solution)/shard_map/ppermute | solution.py:130
  184.6 21.3 %collective-permute-start.22 = (bf16[512,256]{0,1:T(8,128)(2,1)}, bf16[512,256]{0,1:T(8,128)(2,1)}, u32[]{:S(2)}, u32[]{:S(2)}) collective-permute-start(bf16[512,256]{0,1:T(8,128)(2,1)} %slice.2796), channel_id=1, source_target_pairs={{0,2},{2,0},{1,3},{3,1},{4,6},{6,4},{5,7},{7,5},{8,10},{10,8},{9,1... | collective-permute-start | bytes 786440 | tf_op jit(solution)/shard_map/ppermute | solution.py:64
  187.8 20.3 %collective-permute-start.21 = (bf16[256,512]{1,0:T(8,128)(2,1)}, bf16[256,512]{1,0:T(8,128)(2,1)}, u32[]{:S(2)}, u32[]{:S(2)}) collective-permute-start(bf16[256,512]{1,0:T(8,128)(2,1)} %slice.2797), channel_id=1, source_target_pairs={{0,2},{2,0},{1,3},{3,1},{4,6},{6,4},{5,7},{7,5},{8,10},{10,8},{9,1... | collective-permute-start | bytes 786440 | tf_op jit(solution)/shard_map/ppermute | solution.py:64
  189.9 3.4 %collective-permute-start.17 = (bf16[1024,128]{1,0:T(8,128)(2,1)}, bf16[1024,128]{1,0:T(8,128)(2,1)}, u32[]{:S(2)}, u32[]{:S(2)}) collective-permute-start(bf16[1024,128]{1,0:T(8,128)(2,1)} %get-tuple-element.160), channel_id=1, source_target_pairs={{0,2},{2,0},{1,3},{3,1},{4,6},{6,4},{5,7},{7,5},{8,10},{10,8},{9,1... | collective-permute-start | bytes 786440 | tf_op jit(solution)/shard_map/ppermute | solution.py:64
  203.9 5.2 %collective-permute-start.37 = (bf16[32,128]{1,0:T(8,128)(2,1)S(1)}, bf16[32,128]{1,0:T(8,128)(2,1)S(1)}, u32[]{:S(2)}, u32[]{:S(2)}) collective-permute-start(bf16[32,128]{1,0:T(8,128)(2,1)S(1)} %fusion.312), channel_id=1, source_target_pairs={{0,4},{4,0},{8,12},{12,8},{1,5},{5,1},{9,13},{13,9},{2,6},{6,2},{1... | collective-permute-start | bytes 24584 | tf_op jit(solution)/shard_map/ppermute | solution.py:130
  209.1 3.7 %collective-permute-start.38 = (bf16[16,128]{1,0:T(8,128)(2,1)S(1)}, bf16[16,128]{1,0:T(8,128)(2,1)S(1)}, u32[]{:S(2)}, u32[]{:S(2)}) collective-permute-start(bf16[16,128]{1,0:T(8,128)(2,1)S(1)} %fusion.318), channel_id=1, source_target_pairs={{0,1},{1,0},{2,3},{3,2},{4,5},{5,4},{6,7},{7,6},{8,9},{9,8},{10,11... | collective-permute-start | bytes 12296 | tf_op jit(solution)/shard_map/ppermute | solution.py:130
  212.8 4.5 %collective-permute-start.39 = (bf16[8,128]{1,0:T(8,128)(2,1)S(1)}, bf16[8,128]{1,0:T(8,128)(2,1)S(1)}, u32[]{:S(2)}, u32[]{:S(2)}) collective-permute-start(bf16[8,128]{1,0:T(8,128)(2,1)S(1)} %fusion.323), channel_id=1, source_target_pairs={{0,8},{4,12},{8,0},{12,4},{1,9},{5,13},{9,1},{13,5},{2,10},{6,14},... | collective-permute-start | bytes 6152 | tf_op jit(solution)/shard_map/ppermute | solution.py:130
  217.3 4.6 %collective-permute-start.40 = (bf16[8,128]{1,0:T(8,128)(2,1)S(1)}, bf16[8,128]{1,0:T(8,128)(2,1)S(1)}, u32[]{:S(2)}, u32[]{:S(2)}) collective-permute-start(bf16[8,128]{1,0:T(8,128)(2,1)S(1)} %fusion.322), channel_id=1, source_target_pairs={{0,8},{4,12},{8,0},{12,4},{1,9},{5,13},{9,1},{13,5},{2,10},{6,14},... | collective-permute-start | bytes 6152 | tf_op jit(solution)/shard_map/ppermute | solution.py:130
  221.9 3.6 %collective-permute-start.41 = (bf16[16,128]{1,0:T(8,128)(2,1)S(1)}, bf16[16,128]{1,0:T(8,128)(2,1)S(1)}, u32[]{:S(2)}, u32[]{:S(2)}) collective-permute-start(bf16[16,128]{1,0:T(8,128)(2,1)S(1)} %maximum_select_fusion.15), channel_id=1, source_target_pairs={{0,1},{1,0},{2,3},{3,2},{4,5},{5,4},{6,7},{7,6},{8,9},{9,8},{10,11... | collective-permute-start | bytes 12296 | tf_op jit(solution)/shard_map/ppermute | solution.py:130
  222.4 11.6 %collective-permute-start.23 = (bf16[512,256]{0,1:T(8,128)(2,1)S(1)}, bf16[512,256]{0,1:T(8,128)(2,1)S(1)}, u32[]{:S(2)}, u32[]{:S(2)}) collective-permute-start(bf16[512,256]{0,1:T(8,128)(2,1)S(1)} %fusion.290), channel_id=1, source_target_pairs={{0,4},{4,0},{8,12},{12,8},{1,5},{5,1},{9,13},{13,9},{2,6},{6,2},{1... | collective-permute-start | bytes 786440 | tf_op jit(solution)/shard_map/ppermute | solution.py:130
  225.5 4.2 %collective-permute-start.42 = (bf16[32,128]{1,0:T(8,128)(2,1)S(1)}, bf16[32,128]{1,0:T(8,128)(2,1)S(1)}, u32[]{:S(2)}, u32[]{:S(2)}) collective-permute-start(bf16[32,128]{1,0:T(8,128)(2,1)S(1)} %maximum_select_fusion.13), channel_id=1, source_target_pairs={{0,4},{4,0},{8,12},{12,8},{1,5},{5,1},{9,13},{13,9},{2,6},{6,2},{1... | collective-permute-start | bytes 24584 | tf_op jit(solution)/shard_map/ppermute | solution.py:130
  225.9 4.5 %collective-permute-start.19 = (bf16[16,12,128]{2,1,0:T(8,128)(2,1)S(1)}, bf16[16,12,128]{2,1,0:T(8,128)(2,1)S(1)}, u32[]{:S(2)}, u32[]{:S(2)}) collective-permute-start(bf16[16,12,128]{2,1,0:T(8,128)(2,1)S(1)} %get-tuple-element.158), channel_id=1, source_target_pairs={{4,0},{8,4},{12,8},{0,12},{5,1},{9,5},{13,9},{1,13},{6,2},{10,6},{... | collective-permute-start | bytes 147464 | tf_op jit(solution)/shard_map/ppermute | solution.py:29
  227.8 6.1 %collective-permute-start.18 = (bf16[16,12,128]{2,1,0:T(8,128)(2,1)S(1)}, bf16[16,12,128]{2,1,0:T(8,128)(2,1)S(1)}, u32[]{:S(2)}, u32[]{:S(2)}) collective-permute-start(bf16[16,12,128]{2,1,0:T(8,128)(2,1)S(1)} %get-tuple-element.159), channel_id=1, source_target_pairs={{0,4},{4,8},{8,12},{12,0},{1,5},{5,9},{9,13},{13,1},{2,6},{6,10},{... | collective-permute-start | bytes 147464 | tf_op jit(solution)/shard_map/ppermute | solution.py:28
  234.2 5.1 %collective-permute-start.24 = (bf16[256,256]{0,1:T(8,128)(2,1)S(1)}, bf16[256,256]{0,1:T(8,128)(2,1)S(1)}, u32[]{:S(2)}, u32[]{:S(2)}) collective-permute-start(bf16[256,256]{0,1:T(8,128)(2,1)S(1)} %dynamic-slice_convert_fusion.1), channel_id=1, source_target_pairs={{0,1},{1,0},{2,3},{3,2},{4,5},{5,4},{6,7},{7,6},{8,9},{9,8},{10,11... | collective-permute-start | bytes 393224 | tf_op jit(solution)/shard_map/ppermute | solution.py:130
  234.9 9.8 %collective-permute-start.20 = (bf16[12,152,128]{2,1,0:T(8,128)(2,1)S(1)}, bf16[12,152,128]{2,1,0:T(8,128)(2,1)S(1)}, u32[]{:S(2)}, u32[]{:S(2)}) collective-permute-start(bf16[12,152,128]{2,1,0:T(8,128)(2,1)S(1)} %slice_select_fusion), channel_id=1, source_target_pairs={{0,1},{1,0},{2,3},{3,2},{4,5},{5,4},{6,7},{7,6},{8,9},{9,8},{10,11... | collective-permute-start | bytes 1400840 | tf_op jit(solution)/shard_map/ppermute | solution.py:23
  239.4 5.2 %collective-permute-start.25 = (bf16[128,256]{0,1:T(8,128)(2,1)S(1)}, bf16[128,256]{0,1:T(8,128)(2,1)S(1)}, u32[]{:S(2)}, u32[]{:S(2)}) collective-permute-start(bf16[128,256]{0,1:T(8,128)(2,1)S(1)} %dynamic-slice_convert_fusion.3), channel_id=1, source_target_pairs={{0,8},{4,12},{8,0},{12,4},{1,9},{5,13},{9,1},{13,5},{2,10},{6,14},... | collective-permute-start | bytes 196616 | tf_op jit(solution)/shard_map/ppermute | solution.py:130
  244.6 5.4 %collective-permute-start.26 = (bf16[128,256]{0,1:T(8,128)(2,1)S(1)}, bf16[128,256]{0,1:T(8,128)(2,1)S(1)}, u32[]{:S(2)}, u32[]{:S(2)}) collective-permute-start(bf16[128,256]{0,1:T(8,128)(2,1)S(1)} %add_convert_fusion.3), channel_id=1, source_target_pairs={{0,8},{4,12},{8,0},{12,4},{1,9},{5,13},{9,1},{13,5},{2,10},{6,14},... | collective-permute-start | bytes 196616 | tf_op jit(solution)/shard_map/ppermute | solution.py:130
  250.5 5.0 %collective-permute-start.27 = (bf16[256,256]{0,1:T(8,128)(2,1)S(1)}, bf16[256,256]{0,1:T(8,128)(2,1)S(1)}, u32[]{:S(2)}, u32[]{:S(2)}) collective-permute-start(bf16[256,256]{0,1:T(8,128)(2,1)S(1)} %maximum_select_fusion.11), channel_id=1, source_target_pairs={{0,1},{1,0},{2,3},{3,2},{4,5},{5,4},{6,7},{7,6},{8,9},{9,8},{10,11... | collective-permute-start | bytes 393224 | tf_op jit(solution)/shard_map/ppermute | solution.py:130
  255.6 10.9 %collective-permute-start.28 = (bf16[512,256]{0,1:T(8,128)(2,1)S(1)}, bf16[512,256]{0,1:T(8,128)(2,1)S(1)}, u32[]{:S(2)}, u32[]{:S(2)}) collective-permute-start(bf16[512,256]{0,1:T(8,128)(2,1)S(1)} %maximum_select_fusion.9), channel_id=1, source_target_pairs={{0,4},{4,0},{8,12},{12,8},{1,5},{5,1},{9,13},{13,9},{2,6},{6,2},{1... | collective-permute-start | bytes 786440 | tf_op jit(solution)/shard_map/ppermute | solution.py:130
  (241 other events, 1318.6 us)
where the time goes:
time: 272 us; the launch traced here: 271 us
  other arithmetic  99 us (36%)
  waiting for transfers between devices  79 us (29%)
  starting transfers between devices  40.1 us (15%)
  local copies, waits for them, and re-layouts  25 us (9%)
  matrix products  21.9 us (8%)
  between operations  5.45 us (2%)
    ppermute x24, waiting for transfers between devices, partner(): return lax.ppermute(x, axis, [(i, i ^ dist) for i in range(count)])  48.3 us
    reduce_sum x7, other arithmetic, tap_grads(): results.append(jnp.sum(window.astype(F32) * upstream, axis=(0, 1)))  31.6 us
    dot_general x11, matrix products, dot(): lax.dot_general(a, b, ((contract[0:1], contract[1:2]), ((), ())), preferr...  21.9 us
    ppermute x4, waiting for transfers between devices, halo_stage(): lax.ppermute(jnp.where(index == 0, tail, head), axis, [(0, 1), (1, 0)])  19.9 us
    ppermute x24, starting transfers between devices, partner(): return lax.ppermute(x, axis, [(i, i ^ dist) for i in range(count)])  18.1 us
    ppermute x4, starting transfers between devices, halo_stage(): high = lax.ppermute(head, axis, backward)  12.8 us
    convert_element_type x1, other arithmetic, on_device(): (grad1.astype(F32) + conv(widen(dconv0), kernels[0], True)).astype(BF)  10.4 us
    convert_element_type x1, other arithmetic, on_device(): conv1 = to_cells(conv(widened1, kernels[1], False).astype(BF))  10.4 us
  transfers between devices with their start and end apart: 49, of which 25 were waited for; matrix products, arithmetic and copies ran while one was open for 44% of the time, Pallas kernels for 0%

commit v1 on v0

v1 whole, which is shorter than its diff:
```python
import math

import jax
import jax.numpy as jnp
from jax import lax
from jax.experimental import pallas as pl
from jax.experimental.pallas import tpu as pltpu
from jax.sharding import PartitionSpec as P

BF = jnp.bfloat16
F32 = jnp.float32


TILE = 32


def call(kernel, **kwargs):
    return pl.pallas_call(
        kernel,
        compiler_params=pltpu.CompilerParams(vmem_limit_bytes=48 * 2**20),
        **kwargs,
    )


VM = pl.BlockSpec(memory_space=pltpu.VMEM)
SM = pl.BlockSpec(memory_space=pltpu.SMEM)


def spread(wide, shifted, rows, pieces):
    for first, value in pieces:
        wide[:, first : first + value.shape[1], :] = value[...].astype(F32)
    shifted[...] = wide[:, 4 : 4 + shifted.shape[1], :]


def window(wide, shifted, row, tile, col_tap, cols):
    if col_tap % 2:
        return wide[row, pl.ds(pl.multiple_of(tile * cols + 4 * col_tap + 4, 8), cols), :]
    return shifted[row, pl.ds(pl.multiple_of(tile * cols + 4 * col_tap, 8), cols), :]


def wide_shapes(rows, breadth):
    return [pltpu.VMEM((rows, breadth + 32, 128), F32), pltpu.VMEM((rows, breadth + 24, 128), F32)]


def conv_local(block, low, high, weights):
    rows, breadth, chans = block.shape
    groups = rows // 4

    def kernel(block_ref, low_ref, high_ref, w_ref, out_ref, wide, shifted):
        spread(wide, shifted, rows, ((16, block_ref), (4, low_ref), (16 + breadth, high_ref)))
        tiles = breadth // TILE

        def step(i, carry):
            cls, tile = i // tiles, i % tiles
            sums = [jnp.zeros((TILE // 8, 8, chans), F32) for _ in range(groups)]
            for q in range(7):
                taps = {}
                for r in range(groups):
                    v = window(wide, shifted, 4 * r + cls, tile, q, TILE).reshape(-1, 8, chans)
                    for k in range(groups):
                        p = r - k + 3
                        if 0 <= p <= 6:
                            if p not in taps:
                                taps[p] = w_ref[7 * p + q : 7 * p + q + 1, :]
                            sums[k] = sums[k] + taps[p] * v
            for k in range(groups):
                out_ref[4 * k + cls, pl.ds(pl.multiple_of(tile * TILE, 8), TILE), :] = sums[
                    k
                ].reshape(TILE, chans)
            return carry

        lax.fori_loop(0, 4 * tiles, step, 0)

    return call(
        kernel,
        in_specs=[VM] * 4,
        out_specs=VM,
        out_shape=jax.ShapeDtypeStruct(block.shape, F32),
        scratch_shapes=wide_shapes(rows, breadth),
        name="conv_local",
    )(block, low, high, weights)


def conv_remote(meta, sums_in, got, weights, base=None, last=True):
    rows, breadth, chans = sums_in.shape
    groups = rows // 4
    half = rows // 2

    def kernel(meta_ref, sums_ref, got_ref, w_ref, *rest):
        if base is not None:
            base_ref, rest = rest[0], rest[1:]
        if last:
            out_ref, send_ref, wide, shifted = rest
        else:
            out_ref, wide, shifted = rest
        below = meta_ref[0]
        spread(wide, shifted, 12, ((4, got_ref),))
        tiles = breadth // TILE

        def mirror(x, most):
            return x + below * (most - 2 * x)

        def step(i, carry):
            cls, tile = i // tiles, i % tiles
            cols = pl.ds(pl.multiple_of(tile * TILE, 8), TILE)
            at = [4 * mirror(k, groups - 1) + cls for k in range(groups)]
            sums = [sums_ref[at[k], cols, :].reshape(-1, 8, chans) for k in range(groups)]
            for q in range(7):
                taps = [w_ref[pl.ds(7 * mirror(p, 6) + q, 1), :] for p in range(3)]
                for r in range(3):
                    v = window(wide, shifted, 4 * mirror(r, 2) + cls, tile, q, TILE)
                    v = v.reshape(-1, 8, chans)
                    for k in range(min(groups, r + 1)):
                        sums[k] = sums[k] + taps[r - k] * v
            for k in range(groups):
                value = sums[k].reshape(TILE, chans)
                if base is not None:
                    value = value + base_ref[at[k], cols, :].astype(F32)
                out_ref[at[k], cols, :] = value.astype(out_ref.dtype)
            return carry

        lax.fori_loop(0, 4 * tiles, step, 0)
        if last:
            send_ref[...] = out_ref[pl.ds((1 - meta_ref[1]) * half, half)]

    field = jax.ShapeDtypeStruct((rows, breadth, chans), BF if last else F32)
    part = jax.ShapeDtypeStruct((half, breadth, chans), BF)
    args = (meta, sums_in, got, weights) + (() if base is None else (base,))
    return call(
        kernel,
        in_specs=[SM] + [VM] * (len(args) - 1),
        out_specs=(VM, VM) if last else VM,
        out_shape=(field, part) if last else field,
        scratch_shapes=wide_shapes(12, breadth),
        name="conv_remote",
    )(*args)


def tap_sums(meta, grad, block, low, high, gots):
    rows, breadth, chans = block.shape
    groups = rows // 4
    count = len(gots)

    def kernel(meta_ref, grad_ref, block_ref, low_ref, high_ref, *rest):
        got_refs, (out_ref, g_ref, wide, shifted, rwide, rshifted) = rest[:count], rest[count:]
        g_ref[...] = grad_ref[...].astype(F32)
        spread(wide, shifted, rows, ((16, block_ref), (4, low_ref), (16 + breadth, high_ref)))
        tiles = breadth // 8

        def near(cols_taps):
            def step(i, sums):
                cls, tile = i // tiles, i % tiles
                sums = list(sums)
                cols = pl.ds(pl.multiple_of(tile * 8, 8), 8)
                g = [g_ref[4 * k + cls, cols, :] for k in range(groups)]
                for n, q in enumerate(cols_taps):
                    for r in range(groups):
                        v = window(wide, shifted, 4 * r + cls, tile, q, 8)
                        for k in range(groups):
                            p = r - k + 3
                            if 0 <= p <= 6:
                                sums[7 * n + p] = sums[7 * n + p] + g[k] * v
                return tuple(sums)

            zero = jnp.zeros((8, chans), F32)
            sums = lax.fori_loop(0, 4 * tiles, step, (zero,) * (7 * len(cols_taps)))
            for n, q in enumerate(cols_taps):
                for p in range(7):
                    out_ref[7 * p + q : 7 * p + q + 1, :] = jnp.sum(
                        sums[7 * n + p], axis=0, keepdims=True
                    )

        def far(index, cols_taps):
            below = meta_ref[index]

            def mirror(x, most):
                return x + below * (most - 2 * x)

            def step(i, sums):
                cls, tile = i // tiles, i % tiles
                sums = list(sums)
                cols = pl.ds(pl.multiple_of(tile * 8, 8), 8)
                near_k = range(min(3, groups))
                g = [g_ref[4 * mirror(k, groups - 1) + cls, cols, :] for k in near_k]
                for n, q in enumerate(cols_taps):
                    for r in range(3):
                        v = window(rwide, rshifted, 4 * mirror(r, 2) + cls, tile, q, 8)
                        for k in near_k:
                            if k <= r:
                                sums[3 * n + r - k] = sums[3 * n + r - k] + g[k] * v
                return tuple(sums)

            zero = jnp.zeros((8, chans), F32)
            sums = lax.fori_loop(0, 4 * tiles, step, (zero,) * (3 * len(cols_taps)))
            for n, q in enumerate(cols_taps):
                for p in range(3):
                    at = pl.ds(7 * mirror(p, 6) + q, 1)
                    out_ref[at, :] = out_ref[at, :] + jnp.sum(
                        sums[3 * n + p], axis=0, keepdims=True
                    )

        for cols_taps in ((0, 2, 4, 6), (1, 3, 5)):
            near(cols_taps)
        for index in range(count):
            spread(rwide, rshifted, 12, ((4, got_refs[index]),))
            far(index, tuple(range(7)))

    return call(
        kernel,
        in_specs=[SM] + [VM] * (4 + count),
        out_specs=VM,
        out_shape=jax.ShapeDtypeStruct((49, chans), F32),
        scratch_shapes=[pltpu.VMEM(block.shape, F32)]
        + wide_shapes(rows, breadth)
        + wide_shapes(12, breadth),
        name="tap_sums",
    )(meta, grad, block, low, high, *gots)


CUBIC = 0.044715
ROOT = math.sqrt(2.0 / math.pi)


def layer_norm(x):
    centred = x - jnp.mean(x, axis=-1, keepdims=True)
    inverse = lax.rsqrt(jnp.mean(centred * centred, axis=-1, keepdims=True) + 1e-06)
    return centred * inverse, inverse


def mxu(a, b):
    return jnp.dot(a, b, preferred_element_type=F32)


STEP = 256


def cell_specs(cells, chans):
    steps = cells // STEP
    mine = pl.BlockSpec((STEP, chans), lambda i, meta: (meta[1] * steps + i, 0))
    theirs = pl.BlockSpec((STEP, chans), lambda i, meta: (i, 0))
    return mine, theirs


def fixed(shape):
    return pl.BlockSpec(shape, lambda i, meta: (0,) * len(shape), pipeline_mode=pl.Buffered(1))


def mix_forward(meta, field, other, w_in, w_out, gain):
    cells, chans = other.shape
    hidden = w_in.shape[1]
    mine, theirs = cell_specs(cells, chans)

    def kernel(meta_ref, a_ref, b_ref, wi_ref, wo_ref, gain_ref, own_ref, send_ref):
        x = jnp.concatenate([a_ref[...].astype(F32), b_ref[...].astype(F32)], axis=1)
        y = (layer_norm(x)[0] * gain_ref[...]).astype(BF)
        pre = mxu(y, wi_ref[...])
        tanh = jnp.tanh(pre * (ROOT + (ROOT * CUBIC) * (pre * pre)))
        hid = (pre * (0.5 + 0.5 * tanh)).astype(BF)
        mixed = mxu(hid, wo_ref[...]).astype(BF)
        own_ref[...] = mixed[:, :chans]
        send_ref[...] = mixed[:, chans:]

    return pl.pallas_call(
        kernel,
        grid_spec=pltpu.PrefetchScalarGridSpec(
            num_scalar_prefetch=1,
            grid=(cells // STEP,),
            in_specs=[
                mine,
                theirs,
                fixed((2 * chans, hidden)),
                fixed((hidden, 2 * chans)),
                fixed((1, 2 * chans)),
            ],
            out_specs=[theirs, theirs],
        ),
        out_shape=[jax.ShapeDtypeStruct((cells, chans), BF)] * 2,
        compiler_params=pltpu.CompilerParams(vmem_limit_bytes=48 * 2**20),
        name="mix_forward",
    )(meta, field, other, w_in, w_out, gain)


def mix_backward(meta, field, other, gfield, gother, w_in, w_in_t, w_out_t, gain):
    cells, chans = other.shape
    hidden = w_in.shape[1]
    steps = cells // STEP
    half = hidden // 2
    mine, theirs = cell_specs(cells, chans)

    def kernel(meta_ref, a_ref, b_ref, ga_ref, gb_ref, wi_ref, wit_ref, wot_ref, gain_ref,
               own_ref, send_ref, keep_ref, give_ref, acc_ref):
        i = pl.program_id(0)

        @pl.when(i == 0)
        def _():
            acc_ref[...] = jnp.zeros_like(acc_ref)

        gains = gain_ref[...]
        x = jnp.concatenate([a_ref[...].astype(F32), b_ref[...].astype(F32)], axis=1)
        xhat, inverse = layer_norm(x)
        y = (xhat * gains).astype(BF)
        g = jnp.concatenate([ga_ref[...], gb_ref[...]], axis=1)
        pre = mxu(y, wi_ref[...])
        square = pre * pre
        tanh = jnp.tanh(pre * (ROOT + (ROOT * CUBIC) * square))
        gate = 0.5 + 0.5 * tanh
        act = pre * gate
        slope = gate + (act - act * gate) * (2 * ROOT + (6 * ROOT * CUBIC) * square)
        hid = act.astype(BF)
        dpre = (mxu(g, wot_ref[...]) * slope).astype(BF)
        acc_ref[: 2 * chans] += lax.dot_general(
            y, dpre, (((0,), (0,)), ((), ())), preferred_element_type=F32
        )
        acc_ref[2 * chans :] += lax.dot_general(
            g, hid, (((0,), (0,)), ((), ())), preferred_element_type=F32
        )
        e = mxu(dpre, wit_ref[...]) * gains
        centre = jnp.mean(e, axis=-1, keepdims=True)
        tilt = jnp.mean(e * xhat, axis=-1, keepdims=True)
        dconv = ((e - centre - xhat * tilt) * inverse).astype(BF)
        own_ref[...] = dconv[:, :chans]
        send_ref[...] = dconv[:, chans:]

        @pl.when(i == steps - 1)
        def _():
            me = meta_ref[1]
            for kind in range(2):
                for side in range(2):
                    place = 2 * kind + me + side * (1 - 2 * me)
                    base = (2 * kind + side) * chans
                    keep_ref[place] = acc_ref[base : base + chans, :half]
                    give_ref[place] = acc_ref[base : base + chans, half:].astype(BF)

    grads = pl.BlockSpec((4, chans, half), lambda i, meta: (0, 0, 0))
    return pl.pallas_call(
        kernel,
        grid_spec=pltpu.PrefetchScalarGridSpec(
            num_scalar_prefetch=1,
            grid=(steps,),
            in_specs=[
                mine,
                theirs,
                mine,
                theirs,
                fixed((2 * chans, hidden)),
                fixed((hidden, 2 * chans)),
                fixed((2 * chans, hidden)),
                fixed((1, 2 * chans)),
            ],
            out_specs=[theirs, theirs, grads, grads],
            scratch_shapes=[pltpu.VMEM((4 * chans, hidden), F32)],
        ),
        out_shape=[jax.ShapeDtypeStruct((cells, chans), BF)] * 2
        + [
            jax.ShapeDtypeStruct((4, chans, half), F32),
            jax.ShapeDtypeStruct((4, chans, half), BF),
        ],
        compiler_params=pltpu.CompilerParams(vmem_limit_bytes=56 * 2**20),
        name="mix_backward",
    )(meta, field, other, gfield, gother, w_in, w_in_t, w_out_t, gain)


def lon_halo(block):
    count = lax.axis_size("lon")
    forward = [(i, (i + 1) % count) for i in range(count)]
    backward = [(target, source) for source, target in forward]
    size = block.shape[1]
    low = lax.ppermute(block[:, size - 12 :], "lon", forward)
    high = lax.ppermute(block[:, :12], "lon", backward)
    return low, high


def lat_halo(block, low, high):
    count = lax.axis_size("lat")
    index = lax.axis_index("lat")
    rows = block.shape[0]

    def strip(first):
        parts = [low, block, high]
        return jnp.concatenate(
            [lax.dynamic_slice_in_dim(x, first, 12, 0) for x in parts], axis=1
        )

    if count == 1:
        return []
    if count == 2:
        got = lax.ppermute(strip((1 - index) * (rows - 12)), "lat", [(0, 1), (1, 0)])
        return [((index == 0).astype(jnp.int32), got)]
    down = [(i, i + 1) for i in range(count - 1)]
    up = [(target, source) for source, target in down]
    above = lax.ppermute(strip(rows - 12), "lat", down)
    below = lax.ppermute(strip(0), "lat", up)
    return [(jnp.int32(0), above), (jnp.int32(1), below)]


def halos(block):
    low, high = lon_halo(block)
    return low, high, lat_halo(block, low, high)


def convolve(me, block, halo, weights, base=None):
    low, high, gots = halo
    sums = conv_local(block, low, high, weights)
    if not gots:
        gots = [(jnp.int32(0), jnp.zeros((12, block.shape[1] + 24, block.shape[2]), BF))]
    for n, (below, got) in enumerate(gots):
        last = n == len(gots) - 1
        meta = jnp.stack([below, me])
        sums = conv_remote(meta, sums, got, weights, base if last else None, last)
    return sums


def swap(x):
    return lax.ppermute(x, "ch", [(0, 1), (1, 0)])


def flat(x):
    return x.reshape(-1, x.shape[-1])


def grid_sum(part):
    lon = lax.axis_size("lon")
    lat = lax.axis_size("lat")
    along = [("lon", 2**n) for n in range(lon.bit_length() - 1)]
    across = [("lat", 2**n) for n in range(lat.bit_length() - 1)]
    steps = along[:1] + across + along[1:]

    def partner(x, axis, dist):
        count = lax.axis_size(axis)
        return lax.ppermute(x, axis, [(i, i ^ dist) for i in range(count)])

    for axis, dist in steps:
        bit = (lax.axis_index(axis) // dist) % 2
        half = part.shape[0] // 2
        keep = lax.dynamic_slice_in_dim(part, bit * half, half, 0)
        send = lax.dynamic_slice_in_dim(part, (1 - bit) * half, half, 0)
        part = keep + partner(send.astype(BF), axis, dist).astype(F32)
    part = part.astype(BF)
    for axis, dist in reversed(steps):
        bit = (lax.axis_index(axis) // dist) % 2
        got = partner(part, axis, dist)
        part = jnp.where(bit == 0, jnp.concatenate([part, got]), jnp.concatenate([got, part]))
    return part


def on_device(inputs, cotangent, kernels, gains, w_in, w_out):
    rows, breadth, own = inputs.shape
    cells = rows * breadth // 2
    scaling = 1.0 / math.sqrt(
        rows * lax.axis_size("lat") * breadth * lax.axis_size("lon")
    )
    me = lax.axis_index("ch")
    place = jnp.stack([me, me])

    def own_first(x, axis):
        half = x.shape[axis] // 2
        first = lax.dynamic_slice_in_dim(x, me * half, half, axis)
        second = lax.dynamic_slice_in_dim(x, (1 - me) * half, half, axis)
        return jnp.concatenate([first, second], axis)

    halo0 = halos(inputs)
    w_in_full = own_first(jnp.concatenate([w_in, swap(w_in)], axis=2), 1)
    w_out_full = own_first(jnp.concatenate([w_out, swap(w_out)], axis=1), 2)
    w_in_t = w_in_full.transpose(0, 2, 1)
    w_out_t = w_out_full.transpose(0, 2, 1)
    gains_full = own_first(gains, 1)
    taps = kernels.astype(F32)
    taps_back = taps[:, ::-1]

    def split(field):
        send = lax.dynamic_slice_in_dim(field, (1 - me) * (rows // 2), rows // 2, 0)
        return flat(field), swap(flat(send))

    def join(mine, send):
        theirs = swap(send)
        pair = jnp.where(
            me == 0, jnp.concatenate([mine, theirs]), jnp.concatenate([theirs, mine])
        )
        return pair.reshape(rows, breadth, own)

    def forward(b, block, halo):
        field, send = convolve(me, block, halo, taps[b])
        return flat(field), swap(flat(send))

    def backward(b, conv, grad):
        mine, send, keep, give = mix_backward(
            place, *conv, *grad, w_in_full[b], w_in_t[b], w_out_t[b], gains_full[b : b + 1]
        )
        return join(mine, send), keep, give

    def weight_sums(keep, give):
        half = keep.shape[-1]
        part = keep.reshape(-1, half) + swap(give).reshape(-1, half).astype(F32)
        summed = grid_sum(part).astype(F32) * scaling
        return summed[: 2 * own], summed[2 * own :].T

    def kernel_sums(grad, block, halo):
        low, high, gots = halo
        meta = jnp.stack([below for below, _ in gots] + [me])
        dk = tap_sums(meta, grad, block, low, high, [got for _, got in gots])
        dk = jnp.pad(dk, ((0, 64 - dk.shape[0]), (0, 0)))
        return grid_sum(dk)[:49].astype(F32) * scaling

    conv0 = forward(0, inputs, halo0)
    grad2 = split(cotangent)
    mixed = mix_forward(place, *conv0, w_in_full[0], w_out_full[0], gains_full[:1])
    current = (inputs.astype(F32) + join(*mixed).astype(F32)).astype(BF)
    halo1 = halos(current)
    conv1 = forward(1, current, halo1)

    dconv1, keep1, give1 = backward(1, conv1, grad2)
    back1 = halos(dconv1)
    gwi1, gwo1 = weight_sums(keep1, give1)
    gk1 = kernel_sums(dconv1, current, halo1)
    grad1, send1 = convolve(me, dconv1, back1, taps_back[1], cotangent)
    dconv0, keep0, give0 = backward(0, conv0, (flat(grad1), swap(flat(send1))))
    back0 = halos(dconv0)
    gwi0, gwo0 = weight_sums(keep0, give0)
    gk0 = kernel_sums(dconv0, inputs, halo0)
    grad0, _ = convolve(me, dconv0, back0, taps_back[0], grad1)
    return (grad0, jnp.stack([gwi0, gwi1]), jnp.stack([gwo0, gwo1]), jnp.stack([gk0, gk1]))


def solution(mesh):
    return jax.shard_map(
        on_device,
        mesh=mesh,
        in_specs=(
            P(("grp", "lat"), "lon", "ch"),
            P(("grp", "lat"), "lon", "ch"),
            P(None, None, "ch"),
            P(),
            P(None, None, "ch"),
            P(None, "ch", None),
        ),
        out_specs=(
            P(("grp", "lat"), "lon", "ch"),
            P("grp", None, "ch"),
            P("grp", "ch", None),
            P("grp", None, "ch"),
        ),
        check_vma=False,
    )
```

time: 272 us -> 211 us (0.78)
  other arithmetic: 99 us -> 17.3 us
  Pallas kernels: 0 us -> 54.5 us
  matrix products: 21.9 us -> 0 us
  waiting for transfers between devices: 79 us -> 71.2 us
  between operations: 5.45 us -> 1.6 us
    pallas_call x0 -> x13, Pallas kernels: none -> 54.5 us  [the longest x2 19.1 us: mix_backward(): pl.pallas_call(kernel, grid_spec=pltpu.PrefetchScalarGridSpec(num_scalar_...]
    convert_element_type x13 -> x2, other arithmetic: 46.7 us -> 0.15 us  [the longest x1 0.15 us: on_device(): current = (inputs.astype(F32) + join(*mixed).astype(F32)).astype(BF)]
    reduce_sum x11 -> x0, other arithmetic: 34.6 us -> none  [the longest x7 31.6 us: tap_grads(): results.append(jnp.sum(window.astype(F32) * upstream, axis=(0, 1)))]
    dot_general x11 -> x0, matrix products: 21.9 us -> none  [dot(): lax.dot_general(a, b, ((contract[0:1], contract[1:2]), ((), ())), preferr...]
    ppermute x12, waiting for transfers between devices: 28.7 us -> 21.7 us  [the longest x4 8.4 us: lon_halo(): low = lax.ppermute(block[:, size - 12:], 'lon', forward)]
    squeeze x0 -> x5, local copies, waits for them, and re-layouts: none -> 6.75 us  [the longest x1 2.16 us: backward(): w_in_full[b]]
    ppermute x24, starting transfers between devices: 18.1 us -> 23.7 us  [partner(): return lax.ppermute(x, axis, [(i, i ^ dist) for i in range(count)])]
    mul x8 -> x2, other arithmetic: 6.49 us -> 1.38 us  [weight_sums(): summed = grid_sum(part).astype(F32) * scaling]
  transfers between devices with their start and end apart: 49 -> 47, of which waited for: 25 -> 25; matrix products, arithmetic and copies ran while one was open for 44% -> 15% of each run, Pallas kernels for 0% -> 16%
where the time goes in v1:
time: 211 us
  waiting for transfers between devices  71.2 us (34%)
  Pallas kernels  54.5 us (26%)
  starting transfers between devices  42.7 us (20%)
  local copies, waits for them, and re-layouts  23.2 us (11%)
  other arithmetic  17.3 us (8%)
    ppermute x24, waiting for transfers between devices, partner(): return lax.ppermute(x, axis, [(i, i ^ dist) for i in range(count)])  46.2 us
    ppermute x24, starting transfers between devices, partner(): return lax.ppermute(x, axis, [(i, i ^ dist) for i in range(count)])  23.7 us
    pallas_call x2, Pallas kernels, mix_backward(): pl.pallas_call(kernel, grid_spec=pltpu.PrefetchScalarGridSpec(num_scalar_...  19.1 us
    pallas_call x2, Pallas kernels, tap_sums(): call(kernel, in_specs=[SM] + [VM] * (4 + count), out_specs=VM, out_shape=...  13.7 us
    unnamed x88, local copies, waits for them, and re-layouts  11.8 us
    pallas_call x4, Pallas kernels, conv_local(): call(kernel, in_specs=[VM] * 4, out_specs=VM, out_shape=jax.ShapeDtypeStr...  9.83 us
    ppermute x4, starting transfers between devices, lon_halo(): high = lax.ppermute(block[:, :12], 'lon', backward)  9.71 us
    ppermute x4, waiting for transfers between devices, lon_halo(): low = lax.ppermute(block[:, size - 12:], 'lon', forward)  8.4 us
  transfers between devices with their start and end apart: 47, of which 25 were waited for; matrix products, arithmetic and copies ran while one was open for 15% of the time, Pallas kernels for 16%

profile of v1, /device:TPU:0, one launch (start us, length us, event | category | flops | bytes accessed | tf_op | source)
XLA Modules:
  0.0 210.5 jit_solution(2208501262693520350)
XLA Ops:
  1.6 5.1 %collective-permute-start.1 = (bf16[16,12,128]{2,1,0:T(8,128)(2,1)S(1)}, bf16[16,12,128]{2,1,0:T(8,128)(2,1)S(1)}, u32[]{:S(2)}, u32[]{:S(2)}) collective-permute-start(bf16[16,12,128]{2,1,0:T(8,128)(2,1)S(1)} %get-tuple-element.62), channel_id=1, source_target_pairs={{4,0},{8,4},{12,8},{0,12},{5,1},{9,5},{13,9},{1,13},{6,2},{10,6},{... | collective-permute-start | bytes 147464 | tf_op jit(solution)/shard_map/ppermute | solution.py:369
  6.7 1.3 copy.14
  9.8 3.0 %collective-permute-done.low_ref = bf16[16,12,128]{2,1,0:T(8,128)(2,1)S(1)} collective-permute-done((bf16[16,12,128]{2,1,0:T(8,128)(2,1)S(1)}, bf16[16,12,128]{2,1,0:T(8,128)(2,1)S(1)}, u32[]{:S(2)}, u32[]{:S(2)}) %collective-permute-start) | collective-permute-done | bytes 49184 | tf_op jit(solution)/shard_map/ppermute | solution.py:368
  12.9 1.6 collective-permute-start.2
  15.9 2.5 %conv_local.4.sums_ref = f32[16,128,128]{2,1,0:T(8,128)S(1)} custom-call(bf16[16,128,128]{2,1,0:T(8,128)(2,1)S(1)} %copy-done, bf16[16,12,128]{2,1,0:T(8,128)(2,1)S(1)} %collective-permute-done.low_ref, bf16[16,12,128]{2,1,0:T(8,128)(2,1)S(1)} %collective-permute-done.1.high_ref, f32[49,128]{1,0:T(8,128)S(1)} %get-tuple-element.65.w_ref), custom_call_target="tpu_custom_call" | custom-call | tf_op jit(solution)/shard_map/conv_local/pallas_call | solution.py:74
  18.4 5.7 %collective-permute-done.2.got_ref.rest_0_ = bf16[12,152,128]{2,1,0:T(8,128)(2,1)S(1)} collective-permute-done((bf16[12,152,128]{2,1,0:T(8,128)(2,1)S(1)}, bf16[12,152,128]{2,1,0:T(8,128)(2,1)S(1)}, u32[]{:S(2)}, u32[]{:S(2)}) %collective-permute-start.2) | collective-permute-done | bytes 466976 | tf_op jit(solution)/shard_map/ppermute | solution.py:387
  24.0 1.7 conv_remote.4
  25.8 1.2 fusion.5
  27.9 1.2 copy.16.wo_ref
  29.2 1.3 fusion.7
  30.5 1.2 fusion.12
  31.8 1.2 copy.15.wi_ref
  33.1 4.2 %mix_forward.1 = (bf16[1024,128]{1,0:T(8,128)(2,1)S(1)}, bf16[1024,128]{1,0:T(8,128)(2,1)}) custom-call(s32[2]{0:T(128)S(1)} %pad_add_fusion.1.meta_ref, bf16[2048,128]{1,0:T(8,128)(2,1)S(1)} %bitcast.66, bf16[1024,128]{1,0:T(8,128)(2,1)S(1)} %collective-permute-done.3.b_ref, bf16[256,1024]{1,0:T(8,128)(2,1)S(1)} %copy.15.wi_ref, ...), custom_call_target="tpu_custom_call" | custom-call | tf_op jit(solution)/shard_map/mix_forward/pallas_call | solution.py:263
  39.5 2.5 %collective-permute-start.8 = (bf16[16,12,128]{2,1,0:T(8,128)(2,1)S(1)}, bf16[16,12,128]{2,1,0:T(8,128)(2,1)S(1)}, u32[]{:S(2)}, u32[]{:S(2)}) collective-permute-start(bf16[16,12,128]{2,1,0:T(8,128)(2,1)S(1)} %get-tuple-element.60), channel_id=1, source_target_pairs={{4,0},{8,4},{12,8},{0,12},{5,1},{9,5},{13,9},{1,13},{6,2},{10,6},{... | collective-permute-start | bytes 147464 | tf_op jit(solution)/shard_map/ppermute | solution.py:369
  42.0 2.4 %collective-permute-done.8.high_ref = bf16[16,12,128]{2,1,0:T(8,128)(2,1)S(1)} collective-permute-done((bf16[16,12,128]{2,1,0:T(8,128)(2,1)S(1)}, bf16[16,12,128]{2,1,0:T(8,128)(2,1)S(1)}, u32[]{:S(2)}, u32[]{:S(2)}) %collective-permute-start.8) | collective-permute-done | bytes 49184 | tf_op jit(solution)/shard_map/ppermute | solution.py:369
  44.4 3.7 %collective-permute-done.7.low_ref = bf16[16,12,128]{2,1,0:T(8,128)(2,1)S(1)} collective-permute-done((bf16[16,12,128]{2,1,0:T(8,128)(2,1)S(1)}, bf16[16,12,128]{2,1,0:T(8,128)(2,1)S(1)}, u32[]{:S(2)}, u32[]{:S(2)}) %collective-permute-start.7) | collective-permute-done | bytes 49184 | tf_op jit(solution)/shard_map/ppermute | solution.py:368
  49.0 1.5 collective-permute-start.9
  51.5 2.2 %copy.17.wi_ref = bf16[256,1024]{1,0:T(8,128)(2,1)} copy(bf16[256,1024]{0,1:T(8,128)(2,1)} %get-tuple-element.50) | data formatting | bytes 1048576 | tf_op jit(solution)/shard_map/squeeze | solution.py:487
  53.8 1.1 copy-done.23
  56.0 2.4 %conv_local.5.sums_ref = f32[16,128,128]{2,1,0:T(8,128)S(1)} custom-call(bf16[16,128,128]{2,1,0:T(8,128)(2,1)S(1)} %fusion.2.block_ref, bf16[16,12,128]{2,1,0:T(8,128)(2,1)S(1)} %collective-permute-done.7.low_ref, bf16[16,12,128]{2,1,0:T(8,128)(2,1)S(1)} %collective-permute-done.8.high_ref, f32[49,128]{1,0:T(8,128)S(1)} %get-tuple-element.66.w_ref), custom_call_target="tpu_custom_call" | custom-call | tf_op jit(solution)/shard_map/conv_local/pallas_call | solution.py:74
  58.4 2.3 %collective-permute-done.9.got_ref.rest_0_ = bf16[12,152,128]{2,1,0:T(8,128)(2,1)S(1)} collective-permute-done((bf16[12,152,128]{2,1,0:T(8,128)(2,1)}, bf16[12,152,128]{2,1,0:T(8,128)(2,1)S(1)}, u32[]{:S(2)}, u32[]{:S(2)}) %collective-permute-start.9) | collective-permute-done | bytes 466976 | tf_op jit(solution)/shard_map/ppermute | solution.py:387
  61.5 1.7 conv_remote.5
  65.5 9.6 %mix_backward.2 = (bf16[1024,128]{1,0:T(8,128)(2,1)}, bf16[1024,128]{1,0:T(8,128)(2,1)}, f32[4,128,512]{2,1,0:T(8,128)}, bf16[4,128,512]{2,1,0:T(8,128)(2,1)}) custom-call(s32[2]{0:T(128)} %copy-done.14, bf16[2048,128]{1,0:T(8,128)(2,1)} %bitcast.68, bf16[1024,128]{1,0:T(8,128)(2,1)} %copy-done.32, bf16[2048,128]{1,0:T(8,128)(2,1)} %bitcast.64, ...), custom_call_target="tpu_custom_call" | custom-call | tf_op jit(solution)/shard_map/mix_backward/pallas_call | solution.py:335
  75.6 1.2 collective-permute-done.12
  76.8 1.2 maximum_select_fusion.1
  78.0 6.8 %tap_sums.3 = f32[49,128]{1,0:T(8,128)S(1)} custom-call(s32[2]{0:T(128)S(1)} %pad_add_fusion.meta_ref, bf16[16,128,128]{2,1,0:T(8,128)(2,1)S(1)} %bitcast.60, bf16[16,128,128]{2,1,0:T(8,128)(2,1)S(1)} %fusion.2.block_ref, bf16[16,12,128]{2,1,0:T(8,128)(2,1)S(1)} %collective-permute-done.7.low_ref, bf16[16,12,128]{2,1,0:T(8,128)(2,1)S(1)} %collective-permute-done.8.high_ref, ...), custom_call_target="tpu_custom_call" | custom-call | tf_op jit(solution)/shard_map/tap_sums/pallas_call | solution.py:208
  85.2 3.4 %collective-permute-done.41 = bf16[32,128]{1,0:T(8,128)(2,1)S(1)} collective-permute-done((bf16[32,128]{1,0:T(8,128)(2,1)S(1)}, bf16[32,128]{1,0:T(8,128)(2,1)S(1)}, u32[]{:S(2)}, u32[]{:S(2)}) %collective-permute-start.41) | collective-permute-done | bytes 8224 | tf_op jit(solution)/shard_map/ppermute | solution.py:430
  88.6 1.6 collective-permute-start.42
  90.9 1.4 collective-permute-start.13
  92.4 2.9 %collective-permute-done.14.high_ref = bf16[16,12,128]{2,1,0:T(8,128)(2,1)S(1)} collective-permute-done((bf16[16,12,128]{2,1,0:T(8,128)(2,1)S(1)}, bf16[16,12,128]{2,1,0:T(8,128)(2,1)S(1)}, u32[]{:S(2)}, u32[]{:S(2)}) %collective-permute-start.14) | collective-permute-done | bytes 49184 | tf_op jit(solution)/shard_map/ppermute | solution.py:369
  95.3 1.7 collective-permute-done.13.low_ref
  100.4 3.9 %collective-permute-done.44 = bf16[8,128]{1,0:T(8,128)(2,1)S(1)} collective-permute-done((bf16[8,128]{1,0:T(8,128)(2,1)S(1)}, bf16[8,128]{1,0:T(8,128)(2,1)S(1)}, u32[]{:S(2)}, u32[]{:S(2)}) %collective-permute-start.44) | collective-permute-done | bytes 2080 | tf_op jit(solution)/shard_map/ppermute | solution.py:430
  104.3 1.5 collective-permute-start.45
  105.8 2.5 %conv_local.6.sums_ref = f32[16,128,128]{2,1,0:T(8,128)S(1)} custom-call(bf16[16,128,128]{2,1,0:T(8,128)(2,1)S(1)} %bitcast.63, bf16[16,12,128]{2,1,0:T(8,128)(2,1)S(1)} %collective-permute-done.13.low_ref, bf16[16,12,128]{2,1,0:T(8,128)(2,1)S(1)} %collective-permute-done.14.high_ref, f32[49,128]{1,0:T(8,128)S(1)} %bitcast.71), custom_call_target="tpu_custom_call" | custom-call | tf_op jit(solution)/shard_map/conv_local/pallas_call | solution.py:74
  109.2 1.2 copy.27
  110.5 1.7 conv_remote.6
  114.7 2.0 collective-permute-start.46
  117.4 9.6 %mix_backward.3 = (bf16[1024,128]{1,0:T(8,128)(2,1)}, bf16[1024,128]{1,0:T(8,128)(2,1)}, f32[4,128,512]{2,1,0:T(8,128)}, bf16[4,128,512]{2,1,0:T(8,128)(2,1)}) custom-call(s32[2]{0:T(128)} %copy-done.14, bf16[2048,128]{1,0:T(8,128)(2,1)} %bitcast.67, bf16[1024,128]{1,0:T(8,128)(2,1)} %copy-done.9, bf16[2048,128]{1,0:T(8,128)(2,1)} %bitcast.65, ...), custom_call_target="tpu_custom_call" | custom-call | tf_op jit(solution)/shard_map/mix_backward/pallas_call | solution.py:335
  128.8 1.2 maximum_select_fusion.2
  130.1 6.8 %tap_sums.2 = f32[49,128]{1,0:T(8,128)S(1)} custom-call(s32[2]{0:T(128)S(1)} %pad_add_fusion.meta_ref, bf16[16,128,128]{2,1,0:T(8,128)(2,1)S(1)} %bitcast.56, bf16[16,128,128]{2,1,0:T(8,128)(2,1)S(1)} %copy-done, bf16[16,12,128]{2,1,0:T(8,128)(2,1)S(1)} %collective-permute-done.low_ref, bf16[16,12,128]{2,1,0:T(8,128)(2,1)S(1)} %collective-permute-done.1.high_ref, ...), custom_call_target="tpu_custom_call" | custom-call | tf_op jit(solution)/shard_map/tap_sums/pallas_call | solution.py:208
  137.2 2.9 %collective-permute-start.31 = (bf16[64,512]{0,1:T(8,128)(2,1)S(1)}, bf16[64,512]{0,1:T(8,128)(2,1)S(1)}, u32[]{:S(2)}, u32[]{:S(2)}) collective-permute-start(bf16[64,512]{0,1:T(8,128)(2,1)S(1)} %dynamic-slice_convert_fusion), channel_id=1, source_target_pairs={{0,8},{4,12},{8,0},{12,4},{1,9},{5,13},{9,1},{13,5},{2,10},{6,14},... | collective-permute-start | bytes 196616 | tf_op jit(solution)/shard_map/ppermute | solution.py:430
  140.7 1.6 collective-permute-start.36
  142.2 4.2 %collective-permute-done.31 = bf16[64,512]{0,1:T(8,128)(2,1)S(1)} collective-permute-done((bf16[64,512]{0,1:T(8,128)(2,1)S(1)}, bf16[64,512]{0,1:T(8,128)(2,1)S(1)}, u32[]{:S(2)}, u32[]{:S(2)}) %collective-permute-start.31) | collective-permute-done | bytes 65568 | tf_op jit(solution)/shard_map/ppermute | solution.py:430
  146.8 2.9 %collective-permute-start.37 = (bf16[8,128]{1,0:T(8,128)(2,1)S(1)}, bf16[8,128]{1,0:T(8,128)(2,1)S(1)}, u32[]{:S(2)}, u32[]{:S(2)}) collective-permute-start(bf16[8,128]{1,0:T(8,128)(2,1)S(1)} %fusion.25), channel_id=1, source_target_pairs={{0,8},{4,12},{8,0},{12,4},{1,9},{5,13},{9,1},{13,5},{2,10},{6,14},... | collective-permute-start | bytes 6152 | tf_op jit(solution)/shard_map/ppermute | solution.py:430
  149.7 5.1 %collective-permute-done.32 = bf16[64,512]{0,1:T(8,128)(2,1)S(1)} collective-permute-done((bf16[64,512]{0,1:T(8,128)(2,1)S(1)}, bf16[64,512]{0,1:T(8,128)(2,1)S(1)}, u32[]{:S(2)}, u32[]{:S(2)}) %collective-permute-start.32) | collective-permute-done | bytes 65568 | tf_op jit(solution)/shard_map/ppermute | solution.py:430
  155.0 1.6 collective-permute-start.33
  156.6 3.8 %collective-permute-done.33 = bf16[128,512]{0,1:T(8,128)(2,1)S(1)} collective-permute-done((bf16[128,512]{0,1:T(8,128)(2,1)S(1)}, bf16[128,512]{0,1:T(8,128)(2,1)S(1)}, u32[]{:S(2)}, u32[]{:S(2)}) %collective-permute-start.33) | collective-permute-done | bytes 131104 | tf_op jit(solution)/shard_map/ppermute | solution.py:430
  162.9 1.8 collective-permute-done.39
  164.7 1.6 collective-permute-start.40
  167.9 1.4 collective-permute-start.19
  170.8 4.3 %collective-permute-done.22 = bf16[256,512]{0,1:T(8,128)(2,1)S(1)} collective-permute-done((bf16[256,512]{0,1:T(8,128)(2,1)}, bf16[256,512]{0,1:T(8,128)(2,1)S(1)}, u32[]{:S(2)}, u32[]{:S(2)}) %collective-permute-start.22) | collective-permute-done | bytes 262176 | tf_op jit(solution)/shard_map/ppermute | solution.py:430
  175.2 1.6 collective-permute-start.23
  177.5 2.8 %collective-permute-done.23 = bf16[128,512]{0,1:T(8,128)(2,1)S(1)} collective-permute-done((bf16[128,512]{0,1:T(8,128)(2,1)S(1)}, bf16[128,512]{0,1:T(8,128)(2,1)S(1)}, u32[]{:S(2)}, u32[]{:S(2)}) %collective-permute-start.23) | collective-permute-done | bytes 131104 | tf_op jit(solution)/shard_map/ppermute | solution.py:430
  180.6 8.6 %collective-permute-done.24 = bf16[64,512]{0,1:T(8,128)(2,1)S(1)} collective-permute-done((bf16[64,512]{0,1:T(8,128)(2,1)S(1)}, bf16[64,512]{0,1:T(8,128)(2,1)S(1)}, u32[]{:S(2)}, u32[]{:S(2)}) %collective-permute-start.24) | collective-permute-done | bytes 65568 | tf_op jit(solution)/shard_map/ppermute | solution.py:430
  189.6 1.7 collective-permute-start.20
  191.3 2.4 %conv_local.7.sums_ref = f32[16,128,128]{2,1,0:T(8,128)S(1)} custom-call(bf16[16,128,128]{2,1,0:T(8,128)(2,1)S(1)} %bitcast.59, bf16[16,12,128]{2,1,0:T(8,128)(2,1)S(1)} %collective-permute-done.18.low_ref, bf16[16,12,128]{2,1,0:T(8,128)(2,1)S(1)} %collective-permute-done.19.high_ref, f32[49,128]{1,0:T(8,128)S(1)} %bitcast.69), custom_call_target="tpu_custom_call" | custom-call | tf_op jit(solution)/shard_map/conv_local/pallas_call | solution.py:74
  193.7 2.4 %collective-permute-done.25 = bf16[64,512]{0,1:T(8,128)(2,1)S(1)} collective-permute-done((bf16[64,512]{0,1:T(8,128)(2,1)S(1)}, bf16[64,512]{0,1:T(8,128)(2,1)S(1)}, u32[]{:S(2)}, u32[]{:S(2)}) %collective-permute-start.25) | collective-permute-done | bytes 65568 | tf_op jit(solution)/shard_map/ppermute | solution.py:430
  196.3 1.6 collective-permute-start.26
  197.8 1.2 convert_multiply_fusion
  199.1 2.2 %collective-permute-done.26 = bf16[128,512]{0,1:T(8,128)(2,1)S(1)} collective-permute-done((bf16[128,512]{0,1:T(8,128)(2,1)S(1)}, bf16[128,512]{0,1:T(8,128)(2,1)S(1)}, u32[]{:S(2)}, u32[]{:S(2)}) %collective-permute-start.26) | collective-permute-done | bytes 131104 | tf_op jit(solution)/shard_map/ppermute | solution.py:430
  201.4 1.3 collective-permute-start.27
  202.8 2.6 %conv_remote.7 = (bf16[16,128,128]{2,1,0:T(8,128)(2,1)}, bf16[8,128,128]{2,1,0:T(8,128)(2,1)}) custom-call(s32[2]{0:T(128)S(1)} %pad_add_fusion.meta_ref, f32[16,128,128]{2,1,0:T(8,128)S(1)} %conv_local.7.sums_ref, bf16[12,152,128]{2,1,0:T(8,128)(2,1)S(1)} %collective-permute-done.20.got_ref, f32[49,128]{1,0:T(8,128)S(1)} %bitcast.70, ...), custom_call_target="tpu_custom_call" | custom-call | tf_op jit(solution)/shard_map/conv_remote/pallas_call | solution.py:129
  205.4 2.5 %collective-permute-done.27 = bf16[256,512]{0,1:T(8,128)(2,1)S(1)} collective-permute-done((bf16[256,512]{0,1:T(8,128)(2,1)S(1)}, bf16[256,512]{0,1:T(8,128)(2,1)S(1)}, u32[]{:S(2)}, u32[]{:S(2)}) %collective-permute-start.27) | collective-permute-done | bytes 262176 | tf_op jit(solution)/shard_map/ppermute | solution.py:430
  208.2 1.3 copy.23
  (220 shorter events, 34.4 us)
Async XLA Ops:
  0.6 7.5 %copy-start.30 = (bf16[2,256,512]{2,1,0:T(8,128)(2,1)S(1)}, bf16[2,256,512]{2,1,0:T(8,128)(2,1)}, u32[]{:S(2)}) copy-start(bf16[2,256,512]{2,1,0:T(8,128)(2,1)} %param.10) | copy-start | bytes 1572868
  1.6 8.2 %collective-permute-start.1 = (bf16[16,12,128]{2,1,0:T(8,128)(2,1)S(1)}, bf16[16,12,128]{2,1,0:T(8,128)(2,1)S(1)}, u32[]{:S(2)}, u32[]{:S(2)}) collective-permute-start(bf16[16,12,128]{2,1,0:T(8,128)(2,1)S(1)} %get-tuple-element.62), channel_id=1, source_target_pairs={{4,0},{8,4},{12,8},{0,12},{5,1},{9,5},{13,9},{1,13},{6,2},{10,6},{... | collective-permute-start | bytes 147464 | tf_op jit(solution)/shard_map/ppermute | solution.py:369
  6.7 6.1 %collective-permute-start = (bf16[16,12,128]{2,1,0:T(8,128)(2,1)S(1)}, bf16[16,12,128]{2,1,0:T(8,128)(2,1)S(1)}, u32[]{:S(2)}, u32[]{:S(2)}) collective-permute-start(bf16[16,12,128]{2,1,0:T(8,128)(2,1)S(1)} %get-tuple-element.63), channel_id=1, source_target_pairs={{0,4},{4,8},{8,12},{12,0},{1,5},{5,9},{9,13},{13,1},{2,6},{6,10},{... | collective-permute-start | bytes 147464 | tf_op jit(solution)/shard_map/ppermute | solution.py:368
  8.1 4.8 %copy-start.26 = (bf16[2,512,256]{1,2,0:T(8,128)(2,1)}, bf16[2,512,256]{1,2,0:T(8,128)(2,1)S(1)}, u32[]{:S(2)}) copy-start(bf16[2,512,256]{1,2,0:T(8,128)(2,1)S(1)} %copy.14) | copy-start | bytes 1572868
  8.1 17.7 %collective-permute-start.5 = (bf16[2,512,256]{1,2,0:T(8,128)(2,1)S(1)}, bf16[2,512,256]{1,2,0:T(8,128)(2,1)}, u32[]{:S(2)}, u32[]{:S(2)}) collective-permute-start(bf16[2,512,256]{1,2,0:T(8,128)(2,1)S(1)} %copy.14), channel_id=1, source_target_pairs={{0,2},{2,0},{1,3},{3,1},{4,6},{6,4},{5,7},{7,5},{8,10},{10,8},{9,1... | collective-permute-start | bytes 1572872 | tf_op jit(solution)/shard_map/ppermute | solution.py:414
  9.2 20.0 %collective-permute-start.4 = (bf16[2,256,512]{1,2,0:T(8,128)(2,1)}, bf16[2,256,512]{1,2,0:T(8,128)(2,1)}, u32[]{:S(2)}, u32[]{:S(2)}) collective-permute-start(bf16[2,256,512]{1,2,0:T(8,128)(2,1)} %copy.12), channel_id=1, source_target_pairs={{0,2},{2,0},{1,3},{3,1},{4,6},{6,4},{5,7},{7,5},{8,10},{10,8},{9,1... | collective-permute-start | bytes 1572872 | tf_op jit(solution)/shard_map/ppermute | solution.py:414
  12.9 11.1 %collective-permute-start.2 = (bf16[12,152,128]{2,1,0:T(8,128)(2,1)S(1)}, bf16[12,152,128]{2,1,0:T(8,128)(2,1)S(1)}, u32[]{:S(2)}, u32[]{:S(2)}) collective-permute-start(bf16[12,152,128]{2,1,0:T(8,128)(2,1)S(1)} %pad_maximum_fusion.4), channel_id=1, source_target_pairs={{0,1},{1,0},{2,3},{3,2},{4,5},{5,4},{6,7},{7,6},{8,9},{9,8},{10,11... | collective-permute-start | bytes 1400840 | tf_op jit(solution)/shard_map/ppermute | solution.py:387
  14.6 18.5 %copy-start.14 = (s32[2]{0:T(128)}, s32[2]{0:T(128)S(1)}, u32[]{:S(2)}) copy-start(s32[2]{0:T(128)S(1)} %pad_add_fusion.1.meta_ref) | copy-start | bytes 28
  15.2 17.9 %copy-start.13 = (f32[1,256]{1,0:T(1,128)}, f32[1,256]{1,0:T(1,128)S(1)}, u32[]{:S(2)}) copy-start(f32[1,256]{1,0:T(1,128)S(1)} %get-tuple-element.69.gain_ref) | copy-start | bytes 3076
  15.9 40.1 %copy-start.11 = (f32[49,128]{1,0:T(8,128)}, f32[49,128]{1,0:T(8,128)S(1)}, u32[]{:S(2)}) copy-start(f32[49,128]{1,0:T(8,128)S(1)} %get-tuple-element.66.w_ref) | copy-start | bytes 75268
  18.4 7.4 %copy-start.27 = (bf16[2,512,256]{1,2,0:T(8,128)(2,1)S(1)}, bf16[2,512,256]{1,2,0:T(8,128)(2,1)}, u32[]{:S(2)}) copy-start(bf16[2,512,256]{1,2,0:T(8,128)(2,1)} %copy-done.26) | copy-start | bytes 1572868
  25.7 7.4 %copy-start.6 = (bf16[16,128,128]{2,1,0:T(8,128)(2,1)}, bf16[16,128,128]{2,1,0:T(8,128)(2,1)S(1)}, u32[]{:S(2)}) copy-start(bf16[16,128,128]{2,1,0:T(8,128)(2,1)S(1)} %get-tuple-element.21) | copy-start | bytes 1572868
  25.7 7.4 %collective-permute-start.3 = (bf16[1024,128]{1,0:T(8,128)(2,1)S(1)}, bf16[1024,128]{1,0:T(8,128)(2,1)S(1)}, u32[]{:S(2)}, u32[]{:S(2)}) collective-permute-start(bf16[1024,128]{1,0:T(8,128)(2,1)S(1)} %bitcast.74), channel_id=1, source_target_pairs={{0,2},{2,0},{1,3},{3,1},{4,6},{6,4},{5,7},{7,5},{8,10},{10,8},{9,1... | collective-permute-start | bytes 786440 | tf_op jit(solution)/shard_map/ppermute | solution.py:414
  33.1 5.4 %copy-start.1 = (bf16[256,1024]{1,0:T(8,128)(2,1)}, bf16[256,1024]{1,0:T(8,128)(2,1)S(1)}, u32[]{:S(2)}) copy-start(bf16[256,1024]{1,0:T(8,128)(2,1)S(1)} %copy.15.wi_ref) | copy-start | bytes 1572868
  33.1 5.4 %copy-start.9 = (bf16[1024,128]{1,0:T(8,128)(2,1)}, bf16[1024,128]{1,0:T(8,128)(2,1)S(1)}, u32[]{:S(2)}) copy-start(bf16[1024,128]{1,0:T(8,128)(2,1)S(1)} %collective-permute-done.3.b_ref) | copy-start | bytes 786436
  37.3 1.8 collective-permute-start.6
  38.5 25.9 %collective-permute-start.11 = (bf16[1024,128]{1,0:T(8,128)(2,1)}, bf16[1024,128]{1,0:T(8,128)(2,1)}, u32[]{:S(2)}, u32[]{:S(2)}) collective-permute-start(bf16[1024,128]{1,0:T(8,128)(2,1)} %bitcast.12), channel_id=1, source_target_pairs={{0,2},{2,0},{1,3},{3,1},{4,6},{6,4},{5,7},{7,5},{8,10},{10,8},{9,1... | collective-permute-start | bytes 786440 | tf_op jit(solution)/shard_map/ppermute | solution.py:414
  39.4 11.1 %copy-start.16 = (bf16[2,1024,128]{1,2,0:T(8,128)(2,1)S(1)}, bf16[2,1024,128]{1,2,0:T(8,128)(2,1)}, u32[]{:S(2)}) copy-start(bf16[2,1024,128]{1,2,0:T(8,128)(2,1)} %copy-done.15) | copy-start | bytes 1572868
  39.4 11.1 %copy-start.18 = (bf16[2,1024,128]{1,2,0:T(8,128)(2,1)S(1)}, bf16[2,1024,128]{1,2,0:T(8,128)(2,1)}, u32[]{:S(2)}) copy-start(bf16[2,1024,128]{1,2,0:T(8,128)(2,1)} %copy-done.17) | copy-start | bytes 1572868
  39.5 4.9 %collective-permute-start.8 = (bf16[16,12,128]{2,1,0:T(8,128)(2,1)S(1)}, bf16[16,12,128]{2,1,0:T(8,128)(2,1)S(1)}, u32[]{:S(2)}, u32[]{:S(2)}) collective-permute-start(bf16[16,12,128]{2,1,0:T(8,128)(2,1)S(1)} %get-tuple-element.60), channel_id=1, source_target_pairs={{4,0},{8,4},{12,8},{0,12},{5,1},{9,5},{13,9},{1,13},{6,2},{10,6},{... | collective-permute-start | bytes 147464 | tf_op jit(solution)/shard_map/ppermute | solution.py:369
  41.9 6.1 %collective-permute-start.7 = (bf16[16,12,128]{2,1,0:T(8,128)(2,1)S(1)}, bf16[16,12,128]{2,1,0:T(8,128)(2,1)S(1)}, u32[]{:S(2)}, u32[]{:S(2)}) collective-permute-start(bf16[16,12,128]{2,1,0:T(8,128)(2,1)S(1)} %get-tuple-element.61), channel_id=1, source_target_pairs={{0,4},{4,8},{8,12},{12,0},{1,5},{5,9},{9,13},{13,1},{2,6},{6,10},{... | collective-permute-start | bytes 147464 | tf_op jit(solution)/shard_map/ppermute | solution.py:368
  49.0 11.8 %collective-permute-start.9 = (bf16[12,152,128]{2,1,0:T(8,128)(2,1)}, bf16[12,152,128]{2,1,0:T(8,128)(2,1)S(1)}, u32[]{:S(2)}, u32[]{:S(2)}) collective-permute-start(bf16[12,152,128]{2,1,0:T(8,128)(2,1)} %pad_maximum_fusion.5), channel_id=1, source_target_pairs={{0,1},{1,0},{2,3},{3,2},{4,5},{5,4},{6,7},{7,6},{8,9},{9,8},{10,11... | collective-permute-start | bytes 1400840 | tf_op jit(solution)/shard_map/ppermute | solution.py:387
  63.2 1.6 collective-permute-start.10
  75.0 1.8 collective-permute-start.12
  75.2 23.2 %collective-permute-start.28 = (bf16[4,128,512]{2,1,0:T(8,128)(2,1)}, bf16[4,128,512]{2,1,0:T(8,128)(2,1)S(1)}, u32[]{:S(2)}, u32[]{:S(2)}) collective-permute-start(bf16[4,128,512]{2,1,0:T(8,128)(2,1)} %get-tuple-element.37), channel_id=1, source_target_pairs={{0,2},{2,0},{1,3},{3,1},{4,6},{6,4},{5,7},{7,5},{8,10},{10,8},{9,1... | collective-permute-start | bytes 1572872 | tf_op jit(solution)/shard_map/ppermute | solution.py:414
  84.9 3.7 %collective-permute-start.41 = (bf16[32,128]{1,0:T(8,128)(2,1)S(1)}, bf16[32,128]{1,0:T(8,128)(2,1)S(1)}, u32[]{:S(2)}, u32[]{:S(2)}) collective-permute-start(bf16[32,128]{1,0:T(8,128)(2,1)S(1)} %fusion.16), channel_id=1, source_target_pairs={{0,4},{4,0},{8,12},{12,8},{1,5},{5,1},{9,13},{13,9},{2,6},{6,2},{1... | collective-permute-start | bytes 24584 | tf_op jit(solution)/shard_map/ppermute | solution.py:430
  85.2 13.2 %copy-start.28 = (f32[4,128,512]{2,1,0:T(8,128)S(1)}, f32[4,128,512]{2,1,0:T(8,128)}, u32[]{:S(2)}) copy-start(f32[4,128,512]{2,1,0:T(8,128)} %get-tuple-element.36) | copy-start | bytes 3145732
  88.6 3.7 %collective-permute-start.42 = (bf16[16,128]{1,0:T(8,128)(2,1)S(1)}, bf16[16,128]{1,0:T(8,128)(2,1)S(1)}, u32[]{:S(2)}, u32[]{:S(2)}) collective-permute-start(bf16[16,128]{1,0:T(8,128)(2,1)S(1)} %fusion.22), channel_id=1, source_target_pairs={{0,1},{1,0},{2,3},{3,2},{4,5},{5,4},{6,7},{7,6},{8,9},{9,8},{10,11... | collective-permute-start | bytes 12296 | tf_op jit(solution)/shard_map/ppermute | solution.py:430
  90.2 5.0 %collective-permute-start.14 = (bf16[16,12,128]{2,1,0:T(8,128)(2,1)S(1)}, bf16[16,12,128]{2,1,0:T(8,128)(2,1)S(1)}, u32[]{:S(2)}, u32[]{:S(2)}) collective-permute-start(bf16[16,12,128]{2,1,0:T(8,128)(2,1)S(1)} %get-tuple-element.58), channel_id=1, source_target_pairs={{4,0},{8,4},{12,8},{0,12},{5,1},{9,5},{13,9},{1,13},{6,2},{10,6},{... | collective-permute-start | bytes 147464 | tf_op jit(solution)/shard_map/ppermute | solution.py:369
  90.9 6.1 %collective-permute-start.13 = (bf16[16,12,128]{2,1,0:T(8,128)(2,1)S(1)}, bf16[16,12,128]{2,1,0:T(8,128)(2,1)S(1)}, u32[]{:S(2)}, u32[]{:S(2)}) collective-permute-start(bf16[16,12,128]{2,1,0:T(8,128)(2,1)S(1)} %get-tuple-element.59), channel_id=1, source_target_pairs={{0,4},{4,8},{8,12},{12,0},{1,5},{5,9},{9,13},{13,1},{2,6},{6,10},{... | collective-permute-start | bytes 147464 | tf_op jit(solution)/shard_map/ppermute | solution.py:368
  92.3 7.3 %collective-permute-start.43 = (bf16[8,128]{1,0:T(8,128)(2,1)S(1)}, bf16[8,128]{1,0:T(8,128)(2,1)S(1)}, u32[]{:S(2)}, u32[]{:S(2)}) collective-permute-start(bf16[8,128]{1,0:T(8,128)(2,1)S(1)} %fusion.28), channel_id=1, source_target_pairs={{0,8},{4,12},{8,0},{12,4},{1,9},{5,13},{9,1},{13,5},{2,10},{6,14},... | collective-permute-start | bytes 6152 | tf_op jit(solution)/shard_map/ppermute | solution.py:430
  97.9 12.5 %collective-permute-start.15 = (bf16[12,152,128]{2,1,0:T(8,128)(2,1)}, bf16[12,152,128]{2,1,0:T(8,128)(2,1)S(1)}, u32[]{:S(2)}, u32[]{:S(2)}) collective-permute-start(bf16[12,152,128]{2,1,0:T(8,128)(2,1)} %pad_maximum_fusion.6), channel_id=1, source_target_pairs={{0,1},{1,0},{2,3},{3,2},{4,5},{5,4},{6,7},{7,6},{8,9},{9,8},{10,11... | collective-permute-start | bytes 1400840 | tf_op jit(solution)/shard_map/ppermute | solution.py:387
  98.6 7.2 %copy-start.24 = (f32[4,128,512]{2,1,0:T(8,128)}, f32[4,128,512]{2,1,0:T(8,128)S(1)}, u32[]{:S(2)}) copy-start(f32[4,128,512]{2,1,0:T(8,128)S(1)} %convert_add_fusion.1) | copy-start | bytes 3145732
  99.7 13.3 %collective-permute-start.29 = (bf16[256,512]{0,1:T(8,128)(2,1)}, bf16[256,512]{0,1:T(8,128)(2,1)}, u32[]{:S(2)}, u32[]{:S(2)}) collective-permute-start(bf16[256,512]{0,1:T(8,128)(2,1)} %copy.28), channel_id=1, source_target_pairs={{0,4},{4,0},{8,12},{12,8},{1,5},{5,1},{9,13},{13,9},{2,6},{6,2},{1... | collective-permute-start | bytes 786440 | tf_op jit(solution)/shard_map/ppermute | solution.py:430
  99.7 4.7 %collective-permute-start.44 = (bf16[8,128]{1,0:T(8,128)(2,1)S(1)}, bf16[8,128]{1,0:T(8,128)(2,1)S(1)}, u32[]{:S(2)}, u32[]{:S(2)}) collective-permute-start(bf16[8,128]{1,0:T(8,128)(2,1)S(1)} %fusion.27), channel_id=1, source_target_pairs={{0,8},{4,12},{8,0},{12,4},{1,9},{5,13},{9,1},{13,5},{2,10},{6,14},... | collective-permute-start | bytes 6152 | tf_op jit(solution)/shard_map/ppermute | solution.py:430
  104.3 10.3 %collective-permute-start.45 = (bf16[16,128]{1,0:T(8,128)(2,1)S(1)}, bf16[16,128]{1,0:T(8,128)(2,1)S(1)}, u32[]{:S(2)}, u32[]{:S(2)}) collective-permute-start(bf16[16,128]{1,0:T(8,128)(2,1)S(1)} %maximum_select_fusion.12), channel_id=1, source_target_pairs={{0,1},{1,0},{2,3},{3,2},{4,5},{5,4},{6,7},{7,6},{8,9},{9,8},{10,11... | collective-permute-start | bytes 12296 | tf_op jit(solution)/shard_map/ppermute | solution.py:430
  113.0 3.7 %collective-permute-start.16 = (bf16[1024,128]{1,0:T(8,128)(2,1)S(1)}, bf16[1024,128]{1,0:T(8,128)(2,1)S(1)}, u32[]{:S(2)}, u32[]{:S(2)}) collective-permute-start(bf16[1024,128]{1,0:T(8,128)(2,1)S(1)} %bitcast.73), channel_id=1, source_target_pairs={{0,2},{2,0},{1,3},{3,1},{4,6},{6,4},{5,7},{7,5},{8,10},{10,8},{9,1... | collective-permute-start | bytes 786440 | tf_op jit(solution)/shard_map/ppermute | solution.py:414
  114.0 13.6 %collective-permute-start.30 = (bf16[128,512]{0,1:T(8,128)(2,1)S(1)}, bf16[128,512]{0,1:T(8,128)(2,1)S(1)}, u32[]{:S(2)}, u32[]{:S(2)}) collective-permute-start(bf16[128,512]{0,1:T(8,128)(2,1)S(1)} %dynamic-slice_convert_fusion.1), channel_id=1, source_target_pairs={{0,1},{1,0},{2,3},{3,2},{4,5},{5,4},{6,7},{7,6},{8,9},{9,8},{10,11... | collective-permute-start | bytes 393224 | tf_op jit(solution)/shard_map/ppermute | solution.py:430
  114.7 12.4 %collective-permute-start.46 = (bf16[32,128]{1,0:T(8,128)(2,1)S(1)}, bf16[32,128]{1,0:T(8,128)(2,1)S(1)}, u32[]{:S(2)}, u32[]{:S(2)}) collective-permute-start(bf16[32,128]{1,0:T(8,128)(2,1)S(1)} %maximum_select_fusion.10), channel_id=1, source_target_pairs={{0,4},{4,0},{8,12},{12,8},{1,5},{5,1},{9,13},{13,9},{2,6},{6,2},{1... | collective-permute-start | bytes 24584 | tf_op jit(solution)/shard_map/ppermute | solution.py:430
  127.0 1.8 collective-permute-start.17
  130.0 16.6 %copy-start.39 = (bf16[4,128,512]{2,1,0:T(8,128)(2,1)S(1)}, bf16[4,128,512]{2,1,0:T(8,128)(2,1)}, u32[]{:S(2)}) copy-start(bf16[4,128,512]{2,1,0:T(8,128)(2,1)} %get-tuple-element.35) | copy-start | bytes 1572868
  136.9 29.4 %copy-start.29 = (f32[4,128,512]{2,1,0:T(8,128)S(1)}, f32[4,128,512]{2,1,0:T(8,128)}, u32[]{:S(2)}) copy-start(f32[4,128,512]{2,1,0:T(8,128)} %get-tuple-element.34) | copy-start | bytes 3145732
  136.9 3.7 %collective-permute-start.35 = (bf16[32,128]{1,0:T(8,128)(2,1)S(1)}, bf16[32,128]{1,0:T(8,128)(2,1)S(1)}, u32[]{:S(2)}, u32[]{:S(2)}) collective-permute-start(bf16[32,128]{1,0:T(8,128)(2,1)S(1)} %fusion.14), channel_id=1, source_target_pairs={{0,4},{4,0},{8,12},{12,8},{1,5},{5,1},{9,13},{13,9},{2,6},{6,2},{1... | collective-permute-start | bytes 24584 | tf_op jit(solution)/shard_map/ppermute | solution.py:430
  137.2 9.2 %collective-permute-start.31 = (bf16[64,512]{0,1:T(8,128)(2,1)S(1)}, bf16[64,512]{0,1:T(8,128)(2,1)S(1)}, u32[]{:S(2)}, u32[]{:S(2)}) collective-permute-start(bf16[64,512]{0,1:T(8,128)(2,1)S(1)} %dynamic-slice_convert_fusion), channel_id=1, source_target_pairs={{0,8},{4,12},{8,0},{12,4},{1,9},{5,13},{9,1},{13,5},{2,10},{6,14},... | collective-permute-start | bytes 196616 | tf_op jit(solution)/shard_map/ppermute | solution.py:430
  140.7 6.1 %collective-permute-start.36 = (bf16[16,128]{1,0:T(8,128)(2,1)S(1)}, bf16[16,128]{1,0:T(8,128)(2,1)S(1)}, u32[]{:S(2)}, u32[]{:S(2)}) collective-permute-start(bf16[16,128]{1,0:T(8,128)(2,1)S(1)} %fusion.20), channel_id=1, source_target_pairs={{0,1},{1,0},{2,3},{3,2},{4,5},{5,4},{6,7},{7,6},{8,9},{9,8},{10,11... | collective-permute-start | bytes 12296 | tf_op jit(solution)/shard_map/ppermute | solution.py:430
  146.6 8.2 %collective-permute-start.32 = (bf16[64,512]{0,1:T(8,128)(2,1)S(1)}, bf16[64,512]{0,1:T(8,128)(2,1)S(1)}, u32[]{:S(2)}, u32[]{:S(2)}) collective-permute-start(bf16[64,512]{0,1:T(8,128)(2,1)S(1)} %add_convert_fusion), channel_id=1, source_target_pairs={{0,8},{4,12},{8,0},{12,4},{1,9},{5,13},{9,1},{13,5},{2,10},{6,14},... | collective-permute-start | bytes 196616 | tf_op jit(solution)/shard_map/ppermute | solution.py:430
  146.7 19.6 %collective-permute-start.21 = (bf16[4,128,512]{2,1,0:T(8,128)(2,1)S(1)}, bf16[4,128,512]{2,1,0:T(8,128)(2,1)S(1)}, u32[]{:S(2)}, u32[]{:S(2)}) collective-permute-start(bf16[4,128,512]{2,1,0:T(8,128)(2,1)S(1)} %copy-done.39), channel_id=1, source_target_pairs={{0,2},{2,0},{1,3},{3,1},{4,6},{6,4},{5,7},{7,5},{8,10},{10,8},{9,1... | collective-permute-start | bytes 1572872 | tf_op jit(solution)/shard_map/ppermute | solution.py:414
  146.8 9.7 %collective-permute-start.37 = (bf16[8,128]{1,0:T(8,128)(2,1)S(1)}, bf16[8,128]{1,0:T(8,128)(2,1)S(1)}, u32[]{:S(2)}, u32[]{:S(2)}) collective-permute-start(bf16[8,128]{1,0:T(8,128)(2,1)S(1)} %fusion.25), channel_id=1, source_target_pairs={{0,8},{4,12},{8,0},{12,4},{1,9},{5,13},{9,1},{13,5},{2,10},{6,14},... | collective-permute-start | bytes 6152 | tf_op jit(solution)/shard_map/ppermute | solution.py:430
  155.0 5.5 %collective-permute-start.33 = (bf16[128,512]{0,1:T(8,128)(2,1)S(1)}, bf16[128,512]{0,1:T(8,128)(2,1)S(1)}, u32[]{:S(2)}, u32[]{:S(2)}) collective-permute-start(bf16[128,512]{0,1:T(8,128)(2,1)S(1)} %maximum_select_fusion.8), channel_id=1, source_target_pairs={{0,1},{1,0},{2,3},{3,2},{4,5},{5,4},{6,7},{7,6},{8,9},{9,8},{10,11... | collective-permute-start | bytes 393224 | tf_op jit(solution)/shard_map/ppermute | solution.py:430
  156.5 4.5 %collective-permute-start.38 = (bf16[8,128]{1,0:T(8,128)(2,1)S(1)}, bf16[8,128]{1,0:T(8,128)(2,1)S(1)}, u32[]{:S(2)}, u32[]{:S(2)}) collective-permute-start(bf16[8,128]{1,0:T(8,128)(2,1)S(1)} %fusion.24), channel_id=1, source_target_pairs={{0,8},{4,12},{8,0},{12,4},{1,9},{5,13},{9,1},{13,5},{2,10},{6,14},... | collective-permute-start | bytes 6152 | tf_op jit(solution)/shard_map/ppermute | solution.py:430
  160.5 37.3 %collective-permute-start.34 = (bf16[256,512]{0,1:T(8,128)(2,1)S(1)}, bf16[256,512]{0,1:T(8,128)(2,1)}, u32[]{:S(2)}, u32[]{:S(2)}) collective-permute-start(bf16[256,512]{0,1:T(8,128)(2,1)S(1)} %maximum_select_fusion.6), channel_id=1, source_target_pairs={{0,4},{4,0},{8,12},{12,8},{1,5},{5,1},{9,13},{13,9},{2,6},{6,2},{1... | collective-permute-start | bytes 786440 | tf_op jit(solution)/shard_map/ppermute | solution.py:430
  161.1 3.6 %collective-permute-start.39 = (bf16[16,128]{1,0:T(8,128)(2,1)S(1)}, bf16[16,128]{1,0:T(8,128)(2,1)S(1)}, u32[]{:S(2)}, u32[]{:S(2)}) collective-permute-start(bf16[16,128]{1,0:T(8,128)(2,1)S(1)} %maximum_select_fusion.11), channel_id=1, source_target_pairs={{0,1},{1,0},{2,3},{3,2},{4,5},{5,4},{6,7},{7,6},{8,9},{9,8},{10,11... | collective-permute-start | bytes 12296 | tf_op jit(solution)/shard_map/ppermute | solution.py:430
  164.7 5.2 %collective-permute-start.40 = (bf16[32,128]{1,0:T(8,128)(2,1)S(1)}, bf16[32,128]{1,0:T(8,128)(2,1)S(1)}, u32[]{:S(2)}, u32[]{:S(2)}) collective-permute-start(bf16[32,128]{1,0:T(8,128)(2,1)S(1)} %maximum_select_fusion.9), channel_id=1, source_target_pairs={{0,4},{4,0},{8,12},{12,8},{1,5},{5,1},{9,13},{13,9},{2,6},{6,2},{1... | collective-permute-start | bytes 24584 | tf_op jit(solution)/shard_map/ppermute | solution.py:430
  167.4 7.7 %collective-permute-start.22 = (bf16[256,512]{0,1:T(8,128)(2,1)}, bf16[256,512]{0,1:T(8,128)(2,1)S(1)}, u32[]{:S(2)}, u32[]{:S(2)}) collective-permute-start(bf16[256,512]{0,1:T(8,128)(2,1)} %copy.26), channel_id=1, source_target_pairs={{0,4},{4,0},{8,12},{12,8},{1,5},{5,1},{9,13},{13,9},{2,6},{6,2},{1... | collective-permute-start | bytes 786440 | tf_op jit(solution)/shard_map/ppermute | solution.py:430
  167.9 9.6 %collective-permute-start.19 = (bf16[16,12,128]{2,1,0:T(8,128)(2,1)}, bf16[16,12,128]{2,1,0:T(8,128)(2,1)S(1)}, u32[]{:S(2)}, u32[]{:S(2)}) collective-permute-start(bf16[16,12,128]{2,1,0:T(8,128)(2,1)} %get-tuple-element.56), channel_id=1, source_target_pairs={{4,0},{8,4},{12,8},{0,12},{5,1},{9,5},{13,9},{1,13},{6,2},{10,6},{... | collective-permute-start | bytes 147464 | tf_op jit(solution)/shard_map/ppermute | solution.py:369
  169.3 11.3 %collective-permute-start.18 = (bf16[16,12,128]{2,1,0:T(8,128)(2,1)}, bf16[16,12,128]{2,1,0:T(8,128)(2,1)S(1)}, u32[]{:S(2)}, u32[]{:S(2)}) collective-permute-start(bf16[16,12,128]{2,1,0:T(8,128)(2,1)} %get-tuple-element.57), channel_id=1, source_target_pairs={{0,4},{4,8},{8,12},{12,0},{1,5},{5,9},{9,13},{13,1},{2,6},{6,10},{... | collective-permute-start | bytes 147464 | tf_op jit(solution)/shard_map/ppermute | solution.py:368
  170.8 6.0 %copy-start.33 = (f32[1,49,128]{2,1,0:T(8,128)S(1)}, f32[1,49,128]{2,1,0:T(8,128)}, u32[]{:S(2)}) copy-start(f32[1,49,128]{2,1,0:T(8,128)} %multiply_bitcast_fusion) | copy-start | bytes 75268
  170.8 6.0 %copy-start.34 = (f32[1,49,128]{2,1,0:T(8,128)S(1)}, f32[1,49,128]{2,1,0:T(8,128)}, u32[]{:S(2)}) copy-start(f32[1,49,128]{2,1,0:T(8,128)} %multiply_bitcast_fusion.1) | copy-start | bytes 75268
  175.2 5.0 %collective-permute-start.23 = (bf16[128,512]{0,1:T(8,128)(2,1)S(1)}, bf16[128,512]{0,1:T(8,128)(2,1)S(1)}, u32[]{:S(2)}, u32[]{:S(2)}) collective-permute-start(bf16[128,512]{0,1:T(8,128)(2,1)S(1)} %dynamic-slice_convert_fusion.3), channel_id=1, source_target_pairs={{0,1},{1,0},{2,3},{3,2},{4,5},{5,4},{6,7},{7,6},{8,9},{9,8},{10,11... | collective-permute-start | bytes 393224 | tf_op jit(solution)/shard_map/ppermute | solution.py:430
  180.4 8.8 %collective-permute-start.24 = (bf16[64,512]{0,1:T(8,128)(2,1)S(1)}, bf16[64,512]{0,1:T(8,128)(2,1)S(1)}, u32[]{:S(2)}, u32[]{:S(2)}) collective-permute-start(bf16[64,512]{0,1:T(8,128)(2,1)S(1)} %dynamic-slice_convert_fusion.2), channel_id=1, source_target_pairs={{0,8},{4,12},{8,0},{12,4},{1,9},{5,13},{9,1},{13,5},{2,10},{6,14},... | collective-permute-start | bytes 196616 | tf_op jit(solution)/shard_map/ppermute | solution.py:430
  189.4 6.8 %collective-permute-start.25 = (bf16[64,512]{0,1:T(8,128)(2,1)S(1)}, bf16[64,512]{0,1:T(8,128)(2,1)S(1)}, u32[]{:S(2)}, u32[]{:S(2)}) collective-permute-start(bf16[64,512]{0,1:T(8,128)(2,1)S(1)} %add_convert_fusion.1), channel_id=1, source_target_pairs={{0,8},{4,12},{8,0},{12,4},{1,9},{5,13},{9,1},{13,5},{2,10},{6,14},... | collective-permute-start | bytes 196616 | tf_op jit(solution)/shard_map/ppermute | solution.py:430
  189.6 13.2 %collective-permute-start.20 = (bf16[12,152,128]{2,1,0:T(8,128)(2,1)S(1)}, bf16[12,152,128]{2,1,0:T(8,128)(2,1)S(1)}, u32[]{:S(2)}, u32[]{:S(2)}) collective-permute-start(bf16[12,152,128]{2,1,0:T(8,128)(2,1)S(1)} %pad_maximum_fusion.7), channel_id=1, source_target_pairs={{0,1},{1,0},{2,3},{3,2},{4,5},{5,4},{6,7},{7,6},{8,9},{9,8},{10,11... | collective-permute-start | bytes 1400840 | tf_op jit(solution)/shard_map/ppermute | solution.py:387
  196.3 5.0 %collective-permute-start.26 = (bf16[128,512]{0,1:T(8,128)(2,1)S(1)}, bf16[128,512]{0,1:T(8,128)(2,1)S(1)}, u32[]{:S(2)}, u32[]{:S(2)}) collective-permute-start(bf16[128,512]{0,1:T(8,128)(2,1)S(1)} %maximum_select_fusion.7), channel_id=1, source_target_pairs={{0,1},{1,0},{2,3},{3,2},{4,5},{5,4},{6,7},{7,6},{8,9},{9,8},{10,11... | collective-permute-start | bytes 393224 | tf_op jit(solution)/shard_map/ppermute | solution.py:430
  201.4 6.4 %collective-permute-start.27 = (bf16[256,512]{0,1:T(8,128)(2,1)S(1)}, bf16[256,512]{0,1:T(8,128)(2,1)S(1)}, u32[]{:S(2)}, u32[]{:S(2)}) collective-permute-start(bf16[256,512]{0,1:T(8,128)(2,1)S(1)} %maximum_select_fusion.5), channel_id=1, source_target_pairs={{0,4},{4,0},{8,12},{12,8},{1,5},{5,1},{9,13},{13,9},{2,6},{6,2},{1... | collective-permute-start | bytes 786440 | tf_op jit(solution)/shard_map/ppermute | solution.py:430
  (23 other events, 46.1 us)
